TPU v7x, 32 devices: a whole 2x2x4 slice. The times are simulated.
32 devices in a mesh: seq: 8 (over z, y), samp: 4 (over x, core).
Axes of the slice: x: 2, y: 2, z: 4, core: 2. Of those that a mesh axis runs over, the one named last changes fastest.
Arguments:
- atoms: bfloat16 [48, 4096, 128], P('samp', 'seq'), may hold values from -3 to 3
- gain: float32 [128], replicated, may hold values from 0.25 to 1.75
- w_query: bfloat16 [128, 128], replicated, may hold values from -0.5 to 0.5
- w_key: bfloat16 [128, 128], replicated, may hold values from -0.5 to 0.5
- w_value: bfloat16 [128, 128], replicated, may hold values from -0.5 to 0.5
- w_gate: bfloat16 [128, 128], replicated, may hold values from -0.5 to 0.5
- w_out: bfloat16 [128, 128], replicated, may hold values from -0.5 to 0.5
- w_token: bfloat16 [128, 768], replicated, may hold values from -0.5 to 0.5
- w_pair: bfloat16 [16, 4], replicated, may hold values from -1.5 to 1.5
- pair_cond: bfloat16 [128, 32, 2048], P('seq'), may hold values from -6 to 6
- counts: int32 [8], replicated, may hold values from 472 to 512, as said below
- membership: int32 [4096], P('seq'), may hold values from 0 to 383, as said below
- pooled_cot: bfloat16 [48, 384, 768], P('samp', 'seq'), may hold values from -6 to 6
Outputs:
- pooled: bfloat16 [48, 384, 768], P('samp', 'seq')
- grad_atoms: bfloat16 [48, 4096, 128], P('samp', 'seq')
- grad_gain: float32 [128], replicated
- grad_query: float32 [128, 128], replicated
- grad_key: float32 [128, 128], replicated
- grad_value: float32 [128, 128], replicated
- grad_gate: float32 [128, 128], replicated
- grad_out: float32 [128, 128], replicated
- grad_token: float32 [128, 768], replicated
- grad_pair: float32 [16, 4], replicated
Inputs may be any that keep to these rules, and one draw needn't show every extreme that they name: `counts`: live atoms fill the first slots of each shard; some shard is full. `membership`: slots of shard s name tokens s * 48 to (s + 1) * 48 - 1, never falling along the slots; every token has one or more live atoms; slots past the shard's count name its last token.
All inputs are finite; a program needn't handle non-finite values.
Results may differ from a plain program's by a relative error of at most 0.012.
Values may be sent and summed in bfloat16 or wider, within the bound.
A program may use at most 128 MiB of HBM per device.

v0:
```python
import functools

import jax
import jax.numpy as jnp
from jax import lax
from jax.experimental import pallas as pl
from jax.experimental.pallas import tpu as pltpu
from jax.sharding import PartitionSpec as P

HEADS = 4
QBLK = 32
KWIN = 128
LOG2E = 1.4426950408889634

epsilon = 1e-05
F32 = jnp.float32
BF16 = jnp.bfloat16
NN = (((1,), (0,)), ((), ()))
NT = (((1,), (1,)), ((), ()))
TN = (((0,), (0,)), ((), ()))
GROUP = 4
LANES = 128


def mm(a, b, dims=NN):
    return lax.dot_general(a, b, dims, preferred_element_type=F32)


def sigmoid(x):
    return 0.5 * jnp.tanh(0.5 * x) + 0.5


def layer_norm(x, gain):
    centred = x - jnp.mean(x, axis=-1, keepdims=True)
    variance = jnp.mean(centred * centred, axis=-1, keepdims=True)
    inv_std = lax.rsqrt(variance + epsilon)
    normed = centred * inv_std
    return normed, inv_std, (normed * gain).astype(BF16)


def head_lanes(width):
    lane = lax.broadcasted_iota(jnp.int32, (1, width), 1)
    return lane // (width // HEADS)


def expand(block, masks):
    return jnp.concatenate([block * m for m in masks], axis=0)


def collapse(wide, lane_head):
    rows = wide.shape[0] // HEADS
    out = wide[:rows]
    for h in range(1, HEADS):
        out = jnp.where(lane_head == h, wide[h * rows : (h + 1) * rows], out)
    return out


def lane_swap(parts, lane_block):
    count = len(parts)
    outs = []
    for b in range(count):
        out = None
        for a in range(count):
            shift = (QBLK * (a - b)) % LANES
            moved = parts[a] if shift == 0 else pltpu.roll(parts[a], shift, 1)
            out = moved if out is None else jnp.where(lane_block == a, moved, out)
        outs.append(out)
    return outs


def build_bias(counts_ref, pair_ref, wsm_ref, bias_scr, blocks, rows):
    pos = lax.axis_index("seq")
    size = lax.axis_size("seq")
    own = counts_ref[pos]
    left = jnp.where(pos > 0, counts_ref[jnp.maximum(pos - 1, 0)], 0)
    right = jnp.where(pos < size - 1, counts_ref[jnp.minimum(pos + 1, size - 1)], 0)
    rim = (KWIN - QBLK) // 2
    lane_block = head_lanes(LANES)
    chunk = wsm_ref.shape[1]
    per = wsm_ref.shape[0] // HEADS
    wsm = wsm_ref[...]
    for kk in range(pair_ref.shape[1] // chunk):
        biased = mm(wsm, pair_ref[:, kk * chunk : (kk + 1) * chunk], NT)
        for g in range(blocks // GROUP):
            parts = [
                biased[h * per : (h + 1) * per, g * LANES : (g + 1) * LANES] for h in range(HEADS)
            ]
            for w, out in enumerate(lane_swap(parts, lane_block)):
                b = g * GROUP + w
                slot = (
                    lax.broadcasted_iota(jnp.int32, (per, LANES), 0) + kk * per + b * QBLK - rim
                )
                alive = (
                    ((slot < 0) & (slot + rows < left))
                    | ((slot >= 0) & (slot < own))
                    | ((slot >= rows) & (slot - rows < right))
                )
                bias_scr[b, kk * per : (kk + 1) * per, :] = jnp.where(alive, out * LOG2E, -1e30)


def pair_gradient(pair_ref, score_scr, rsum_ref, blocks):
    lane_block = head_lanes(LANES)
    per = rsum_ref.shape[0] // HEADS
    chunk = rsum_ref.shape[1]
    total = None
    for kk in range(pair_ref.shape[1] // chunk):
        columns = []
        for g in range(blocks // GROUP):
            parts = [score_scr[g * GROUP + w, kk * per : (kk + 1) * per, :] for w in range(GROUP)]
            columns.append(jnp.concatenate(lane_swap(parts, lane_block), axis=0))
        grads = jnp.concatenate(columns, axis=1).astype(BF16)
        part = mm(grads, pair_ref[:, kk * chunk : (kk + 1) * chunk])
        total = part if total is None else total + part
    rsum_ref[...] = total


def main_kernel(
    counts_ref,
    atoms_ref,
    low_ref,
    high_ref,
    gain_ref,
    wq_ref,
    wk_ref,
    wv_ref,
    wg_ref,
    wo_ref,
    wt_ref,
    wsm_ref,
    pair_ref,
    ids_ref,
    cot_ref,
    pooled_ref,
    gupd_ref,
    dq_ref,
    dkv_ref,
    edge_low_ref,
    edge_high_ref,
    dg_ref,
    gout_ref,
    gtok_ref,
    rsum_ref,
    bias_scr,
    score_scr,
    member_scr,
    member_t_scr,
    inv_scr,
    wqg_scr,
    wkv_scr,
    hid_scr,
    q_scr,
    gate_scr,
    kv_scr,
    p_scr,
    plow_scr,
    att_scr,
    gatt_scr,
    acc_scr,
):
    step = pl.program_id(0)
    rows, width = q_scr.shape
    blocks = rows // QBLK
    rim = (KWIN - QBLK) // 2
    tokens = inv_scr.shape[0]
    scaling = (width // HEADS) ** (-0.5)
    lane_head = head_lanes(width)
    masks = [(lane_head == h).astype(F32).astype(BF16) for h in range(HEADS)]

    @pl.when(step == 0)
    def _():
        pos = lax.axis_index("seq")
        build_bias(counts_ref, pair_ref, wsm_ref, bias_scr, blocks, rows)
        token = lax.broadcasted_iota(jnp.int32, (tokens, rows), 0)
        slot = lax.broadcasted_iota(jnp.int32, (tokens, rows), 1)
        hit = (ids_ref[...] - pos * tokens == token) & (slot < counts_ref[pos])
        member_t = jnp.where(hit, 1.0, 0.0).astype(F32)
        inv_scr[...] = 1.0 / jnp.sum(member_t, axis=1, keepdims=True)
        member_t_scr[...] = member_t.astype(BF16)
        member_scr[...] = member_t.T.astype(BF16)
        wqg_scr[:, :width] = wq_ref[...]
        wqg_scr[:, width:] = wg_ref[...]
        wkv_scr[:, :width] = wk_ref[...]
        wkv_scr[:, width:] = wv_ref[...]
        score_scr[...] = jnp.zeros_like(score_scr)
        gout_ref[...] = jnp.zeros_like(gout_ref)
        gtok_ref[...] = jnp.zeros_like(gtok_ref)

    gain = gain_ref[...]
    x = atoms_ref[0].astype(F32)
    hid_scr[:rim] = layer_norm(low_ref[0].astype(F32), gain)[2]
    hid_scr[rim : rim + rows] = layer_norm(x, gain)[2]
    hid_scr[rim + rows :] = layer_norm(high_ref[0].astype(F32), gain)[2]
    kv_scr[...] = mm(hid_scr[...], wkv_scr[...]).astype(BF16)
    qg = mm(hid_scr[rim : rim + rows], wqg_scr[...])
    q_scr[...] = qg[:, :width].astype(BF16)
    gate_scr[...] = sigmoid(qg[:, width:])

    for g in range(blocks // GROUP):
        spans = [g * GROUP + w for w in range(GROUP)]
        q_exp = [expand(q_scr[b * QBLK : (b + 1) * QBLK, :], masks) for b in spans]
        scores = [
            mm(kv_scr[b * QBLK : b * QBLK + KWIN, :width], q, NT) for b, q in zip(spans, q_exp)
        ]
        es = [
            jnp.exp2(sc * (scaling * LOG2E) + bias_scr[b]) for b, sc in zip(spans, scores)
        ]
        invs = [1.0 / jnp.sum(e, axis=0, keepdims=True) for e in es]
        ps = [e * inv for e, inv in zip(es, invs)]
        lows = [p.astype(BF16) for p in ps]
        for b, p, low in zip(spans, ps, lows):
            p_scr[b] = p
            plow_scr[b] = low
        wide = [
            mm(low, kv_scr[b * QBLK : b * QBLK + KWIN, width:], TN)
            for b, low in zip(spans, lows)
        ]
        for b, o in zip(spans, wide):
            att_scr[b * QBLK : (b + 1) * QBLK, :] = collapse(o, lane_head)

    gate = gate_scr[...]
    att = att_scr[...]
    gated = (gate * att).astype(BF16)
    updated = (x + mm(gated, wo_ref[...])).astype(BF16)
    chunk = 256
    half = rows // 2
    scaled_cot = (cot_ref[0].astype(F32) * inv_scr[...]).astype(BF16)
    gupd = [None, None]
    for c in range(wt_ref.shape[1] // chunk):
        cols = slice(c * chunk, (c + 1) * chunk)
        wt = wt_ref[:, cols]
        pooled = None
        gtok = None
        for r in range(2):
            span = slice(r * half, (r + 1) * half)
            pre = mm(updated[span], wt)
            sig = sigmoid(pre)
            act = pre * sig
            grad_act = mm(member_scr[span, :], scaled_cot[:, cols])
            grad_pre = (grad_act * (sig + act * (1.0 - sig))).astype(BF16)
            part = mm(member_t_scr[:, span], act.astype(BF16))
            pooled = part if pooled is None else pooled + part
            part = mm(updated[span], grad_pre, TN)
            gtok = part if gtok is None else gtok + part
            part = mm(grad_pre, wt, NT)
            gupd[r] = part if gupd[r] is None else gupd[r] + part
        pooled_ref[0, :, cols] = (pooled * inv_scr[...]).astype(BF16)
        gtok_ref[:, cols] += gtok
    grad_updated = jnp.concatenate(gupd, axis=0).astype(BF16)
    gupd_ref[0] = grad_updated
    gout_ref[...] += mm(gated, grad_updated, TN)
    grad_gate = mm(grad_updated, wo_ref[...], NT) * gate
    gatt_scr[...] = grad_gate.astype(BF16)
    dg_ref[0] = (grad_gate * att * (1.0 - gate)).astype(BF16)

    def tiles(x):
        return [x[n * QBLK : (n + 1) * QBLK] for n in range(KWIN // QBLK)]

    open_k = []
    open_v = []

    def close(first, count):
        for n in range(count):
            at = (first + n) * QBLK
            acc_scr[at : at + QBLK, :width] = open_k[n] * scaling
            acc_scr[at : at + QBLK, width:] = open_v[n]
        del open_k[:count]
        del open_v[:count]

    def merge(opened, parts):
        for n, part in enumerate(parts):
            if n < len(opened):
                opened[n] = opened[n] + part
            else:
                opened.append(part)

    for g in range(blocks // GROUP):
        spans = [g * GROUP + w for w in range(GROUP)]
        g_exp = [expand(gatt_scr[b * QBLK : (b + 1) * QBLK, :], masks) for b in spans]
        gps = [
            mm(kv_scr[b * QBLK : b * QBLK + KWIN, width:], ge, NT) for b, ge in zip(spans, g_exp)
        ]
        dvs = [mm(plow_scr[b], ge) for b, ge in zip(spans, g_exp)]
        ts = [p_scr[b] * gp for b, gp in zip(spans, gps)]
        sums = [jnp.sum(t, axis=0, keepdims=True) for t in ts]
        dss = [t - p_scr[b] * r for b, t, r in zip(spans, ts, sums)]
        lows = [ds.astype(BF16) for ds in dss]
        for b, ds in zip(spans, dss):
            score_scr[b] += ds
        q_exp = [expand(q_scr[b * QBLK : (b + 1) * QBLK, :], masks) for b in spans]
        dks = [mm(low, q) for low, q in zip(lows, q_exp)]
        dqs = [
            mm(low, kv_scr[b * QBLK : b * QBLK + KWIN, :width], TN)
            for b, low in zip(spans, lows)
        ]
        for b, dk, dv in zip(spans, dks, dvs):
            merge(open_k, tiles(dk))
            merge(open_v, tiles(dv))
            close(b, 1)
        for b, dq in zip(spans, dqs):
            dq_ref[0, b * QBLK : (b + 1) * QBLK, :] = (
                collapse(dq, lane_head) * scaling
            ).astype(BF16)
    close(blocks, len(open_k))
    edge_low_ref[0] = acc_scr[:rim].astype(BF16)
    edge_high_ref[0] = acc_scr[rim + rows :].astype(BF16)
    dkv_ref[0] = acc_scr[rim : rim + rows].astype(BF16)

    @pl.when(step == pl.num_programs(0) - 1)
    def _():
        pair_gradient(pair_ref, score_scr, rsum_ref, blocks)


def tail_kernel(
    atoms_ref,
    gain_ref,
    wq_ref,
    wk_ref,
    wv_ref,
    wg_ref,
    gupd_ref,
    dq_ref,
    dkv_ref,
    low_ref,
    high_ref,
    dg_ref,
    gatoms_ref,
    ggain_ref,
    gw_ref,
    d_scr,
    w_scr,
):
    step = pl.program_id(0)
    rows, width = atoms_ref.shape[1:]
    rim = low_ref.shape[1]

    @pl.when(step == 0)
    def _():
        for n, ref in enumerate((wq_ref, wk_ref, wv_ref, wg_ref)):
            w_scr[:, n * width : (n + 1) * width] = ref[...]
        ggain_ref[...] = jnp.zeros_like(ggain_ref)
        gw_ref[...] = jnp.zeros_like(gw_ref)

    gain = gain_ref[...]
    normed, inv_std, hidden = layer_norm(atoms_ref[0].astype(F32), gain)
    d_scr[:, :width] = dq_ref[0]
    d_scr[:, width : 3 * width] = dkv_ref[0]
    d_scr[:, 3 * width :] = dg_ref[0]
    d_scr[:rim, width : 3 * width] = (
        dkv_ref[0, :rim].astype(F32) + low_ref[0].astype(F32)
    ).astype(BF16)
    d_scr[rows - rim :, width : 3 * width] = (
        dkv_ref[0, rows - rim :].astype(F32) + high_ref[0].astype(F32)
    ).astype(BF16)
    d = d_scr[...]
    gw_ref[...] += mm(hidden, d, TN)
    grad_hidden = mm(d, w_scr[...], NT)
    gn = grad_hidden * normed
    ggain_ref[...] += jnp.sum(gn, axis=0, keepdims=True)
    gx = grad_hidden * gain
    grad_ln = inv_std * (
        gx
        - jnp.mean(gx, axis=-1, keepdims=True)
        - normed * jnp.mean(gn * gain, axis=-1, keepdims=True)
    )
    gatoms_ref[0] = (gupd_ref[0].astype(F32) + grad_ln).astype(BF16)


def axis_sizes():
    return [(axis, lax.axis_size(axis)) for axis in ("samp", "seq")]


def sum_kernel(parts, streams, *refs):
    grads = refs[: 5 * parts]
    out_ref, buf, send_sem, recv_sem = refs[5 * parts : 5 * parts + 4]
    slots = refs[5 * parts + 4 :]

    def total(n, *at):
        value = grads[n][at] if at else grads[n][...]
        for p in range(1, parts):
            more = grads[5 * p + n]
            value = value + (more[at] if at else more[...])
        return value

    gtok_ref, rsum_ref = grads[1], grads[3]
    width = grads[0].shape[0]
    axes = axis_sizes()
    peers = sum(size - 1 for _, size in axes)
    sends, recvs = slots[: 2 * streams], slots[2 * streams :]

    def peer(axis, size, distance):
        return lax.rem(lax.axis_index(axis) + distance, size)

    barrier = pltpu.get_barrier_semaphore()
    for axis, size in axes:
        for d in range(1, size):
            pl.semaphore_signal(
                barrier,
                inc=1,
                device_id={axis: peer(axis, size, d)},
                device_id_type=pl.DeviceIdType.MESH,
            )

    every = slice(None)
    blocks = gtok_ref.shape[1] // width
    for n in range(blocks):
        buf[n * width : (n + 1) * width, :] = total(1, every, slice(n * width, (n + 1) * width))
    for n in range(4):
        at = (blocks + n) * width
        buf[at : at + width, :] = total(2, every, slice(n * width, (n + 1) * width))
    at = (blocks + 4) * width
    buf[at : at + width, :] = total(0)
    at += width
    buf[at:, :] = jnp.zeros((buf.shape[0] - at, width), F32)
    high, wide = rsum_ref.shape
    per = high // HEADS
    row = lax.broadcasted_iota(jnp.int32, (high, wide), 0)
    lane = lax.broadcasted_iota(jnp.int32, (high, wide), 1)
    diagonal = jnp.where(lax.rem(row, per) == lane // (wide // per), total(3), 0.0)
    for h in range(HEADS):
        line = jnp.sum(diagonal[h * per : (h + 1) * per], axis=0, keepdims=True)
        for n in range(wide // width):
            buf[at + n * HEADS + h : at + n * HEADS + h + 1, :] = line[
                :, n * width : (n + 1) * width
            ]
    spot = at + HEADS * (wide // width)
    buf[spot : spot + 1, :] = total(4)
    pl.semaphore_wait(barrier, peers)

    unit = buf.shape[0] // streams
    orders = [axes[::-1] if stream % 3 == 1 else axes for stream in range(streams)]
    offs = [stream * unit for stream in range(streams)]
    lengths = [unit] * streams
    pending = [[] for _ in range(streams)]

    def send(stream, src, dst, slot, partner):
        copy = pltpu.make_async_remote_copy(
            src_ref=src,
            dst_ref=dst,
            send_sem=send_sem.at[stream * 2 * peers + slot],
            recv_sem=recv_sem.at[stream * 2 * peers + slot],
            device_id=partner,
            device_id_type=pl.DeviceIdType.MESH,
        )
        copy.start()
        pending[stream].append(copy)

    def absorb(stream, k):
        rows = pl.ds(pl.multiple_of(offs[stream], 16), lengths[stream])
        value = buf[rows, :]
        for n, copy in enumerate(pending[stream]):
            copy.wait()
            value = value + recvs[2 * stream + k][n].astype(F32)
        pending[stream] = []
        return rows, value

    for k in range(2):
        for stream in range(streams):
            axis, size = orders[stream][k]
            base = 0
            if k > 0:
                rows, value = absorb(stream, k - 1)
                buf[rows, :] = value
                base = orders[stream][0][1] - 1
            length = lengths[stream] // size
            for d in range(1, size):
                to = peer(axis, size, d)
                give = pl.multiple_of(offs[stream] + to * length, 16)
                slot = sends[2 * stream + k].at[d - 1]
                slot[...] = buf[pl.ds(give, length), :].astype(BF16)
                send(stream, slot, recvs[2 * stream + k].at[d - 1], base + d - 1, {axis: to})
            lengths[stream] = length
            offs[stream] = offs[stream] + lax.axis_index(axis) * length
    for k in (1, 0):
        for stream in range(streams):
            axis, size = orders[stream][k]
            base = peers
            if k == 1:
                rows, value = absorb(stream, 1)
                out_ref[rows, :] = value.astype(BF16)
            else:
                for copy in pending[stream]:
                    copy.wait()
                pending[stream] = []
                base += orders[stream][1][1] - 1
            length = lengths[stream]
            part = out_ref.at[pl.ds(pl.multiple_of(offs[stream], 16), length), :]
            for d in range(1, size):
                send(stream, part, part, base + d - 1, {axis: peer(axis, size, d)})
            offs[stream] = offs[stream] - lax.axis_index(axis) * length
            lengths[stream] = length * size
    for stream in range(streams):
        for copy in pending[stream]:
            copy.wait()


def unpack_kernel(packed_ref, gq_out, gk_out, gv_out, gg_out, gout_out, gtok_out, small_out):
    width = gout_out.shape[0]
    blocks = gtok_out.shape[1] // width

    def block(n):
        return packed_ref[n * width : (n + 1) * width, :].astype(F32)

    for n in range(blocks):
        gtok_out[:, n * width : (n + 1) * width] = block(n)
    for n, ref in enumerate((gq_out, gk_out, gv_out, gg_out, gout_out)):
        ref[...] = block(blocks + n)
    at = (blocks + 5) * width
    small_out[...] = packed_ref[at : at + small_out.shape[0], :].astype(F32)


def sum_all(halves):
    shape = jax.ShapeDtypeStruct
    gout, gtok, gw = halves[0][:3]
    width = gout.shape[0]
    axes = axis_sizes()
    devices = axes[0][1] * axes[1][1]
    peers = sum(size - 1 for _, size in axes)
    unit = 16 * devices
    lines = gtok.shape[1] + gw.shape[1] + width + 16
    total = -(-lines // unit) * unit
    streams = total // unit
    slots = []
    for stream in range(streams):
        length = unit
        for _, size in axes[::-1] if stream % 3 == 1 else axes:
            length //= size
            slots.append(pltpu.VMEM((size - 1, length, width), BF16))
    operands = [x for half in halves for x in half]
    vmem = pl.BlockSpec(memory_space=pltpu.VMEM)
    packed = pl.pallas_call(
        functools.partial(sum_kernel, len(halves), streams),
        in_specs=[vmem] * len(operands),
        out_specs=vmem,
        out_shape=shape((total, width), BF16),
        scratch_shapes=[
            pltpu.VMEM((total, width), F32),
            pltpu.SemaphoreType.DMA((2 * streams * peers,)),
            pltpu.SemaphoreType.DMA((2 * streams * peers,)),
        ]
        + slots * 2,
        compiler_params=pltpu.CompilerParams(collective_id=0, has_side_effects=True),
    )(*operands)
    return pl.pallas_call(
        unpack_kernel,
        in_specs=[vmem],
        out_specs=[vmem] * 7,
        out_shape=[shape((width, width), F32)] * 5
        + [shape(gtok.shape, F32), shape((16, width), F32)],
    )(packed)


def per_sample(*shape, base=0):
    return pl.BlockSpec((1,) + shape, lambda s: (s + base,) + (0,) * len(shape))


def dropping(kernel, position):
    def body(*refs):
        return kernel(*refs[:position], *refs[position + 1 :])

    return body


def whole(*shape):
    return pl.BlockSpec(shape, lambda s: (0,) * len(shape))


def shifted(block, axis, distance):
    devices = range(lax.axis_size(axis))
    route = [(i - distance, i) for i in devices if i - distance in devices]
    return lax.ppermute(block, axis, route)


def on_device(
    atoms,
    gain,
    w_query,
    w_key,
    w_value,
    w_gate,
    w_out,
    w_token,
    w_pair,
    pair_cond,
    counts,
    membership,
    pooled_cot,
):
    samples, rows, width = atoms.shape
    blocks = rows // QBLK
    rim = (KWIN - QBLK) // 2
    tokens, token_width = pooled_cot.shape[1:]
    channels = w_pair.shape[0]
    per = 2 * LANES // channels
    wsm = (
        w_pair.T[:, None, None, :] * jnp.eye(per, dtype=BF16)[None, :, :, None]
    ).reshape(HEADS * per, per * channels)
    pair2 = pair_cond.reshape(blocks * QBLK, pair_cond.shape[-1])
    gain2 = gain.reshape(1, width)
    ids2 = membership.reshape(1, rows)
    square = whole(width, width)
    params = pltpu.CompilerParams(
        dimension_semantics=("arbitrary",), vmem_limit_bytes=56 * 1024 * 1024
    )
    shape = jax.ShapeDtypeStruct
    anywhere = pl.BlockSpec(memory_space=pl.ANY)

    def run_main(base, count, low, high, before):
        specs = [
            pl.BlockSpec(memory_space=pltpu.SMEM),
            per_sample(rows, width, base=base),
            per_sample(rim, width, base=base),
            per_sample(rim, width, base=base),
            whole(1, width),
            square,
            square,
            square,
            square,
            square,
            whole(width, token_width),
            whole(*wsm.shape),
            whole(*pair2.shape),
            whole(1, rows),
            per_sample(tokens, token_width, base=base),
        ]
        operands = [
            counts,
            atoms,
            low,
            high,
            gain2,
            w_query,
            w_key,
            w_value,
            w_gate,
            w_out,
            w_token,
            wsm,
            pair2,
            ids2,
            pooled_cot,
        ]
        place = len(operands)
        return pl.pallas_call(
            main_kernel if before is None else dropping(main_kernel, place),
            grid=(count,),
            in_specs=specs + ([] if before is None else [anywhere]),
            out_specs=[
                per_sample(tokens, token_width, base=base),
                per_sample(rows, width),
                per_sample(rows, width),
                per_sample(rows, 2 * width),
                per_sample(rim, 2 * width),
                per_sample(rim, 2 * width),
                per_sample(rows, width),
                square,
                whole(width, token_width),
                whole(*wsm.shape),
            ],
            out_shape=[
                shape((samples, tokens, token_width), BF16),
                shape((count, rows, width), BF16),
                shape((count, rows, width), BF16),
                shape((count, rows, 2 * width), BF16),
                shape((count, rim, 2 * width), BF16),
                shape((count, rim, 2 * width), BF16),
                shape((count, rows, width), BF16),
                shape((width, width), F32),
                shape((width, token_width), F32),
                shape(wsm.shape, F32),
            ],
            scratch_shapes=[
                pltpu.VMEM((blocks, KWIN, LANES), F32),
                pltpu.VMEM((blocks, KWIN, LANES), F32),
                pltpu.VMEM((rows, tokens), BF16),
                pltpu.VMEM((tokens, rows), BF16),
                pltpu.VMEM((tokens, 1), F32),
                pltpu.VMEM((width, 2 * width), BF16),
                pltpu.VMEM((width, 2 * width), BF16),
                pltpu.VMEM((rows + 2 * rim, width), BF16),
                pltpu.VMEM((rows, width), BF16),
                pltpu.VMEM((rows, width), F32),
                pltpu.VMEM((rows + 2 * rim, 2 * width), BF16),
                pltpu.VMEM((blocks, KWIN, LANES), F32),
                pltpu.VMEM((blocks, KWIN, LANES), BF16),
                pltpu.VMEM((rows, width), F32),
                pltpu.VMEM((rows, width), BF16),
                pltpu.VMEM((rows + 2 * rim, 2 * width), F32),
            ],
            input_output_aliases={} if before is None else {place: 0},
            cost_estimate=pl.CostEstimate(
                flops=count * rows * 4000000, bytes_accessed=1 << 22, transcendentals=0
            ),
            compiler_params=params,
        )(*operands, *([] if before is None else [before]))

    def run_tail(base, count, gupd, dq, dkv, from_left, from_right, dg, before):
        operands = [
            atoms,
            gain2,
            w_query,
            w_key,
            w_value,
            w_gate,
            gupd,
            dq,
            dkv,
            from_left,
            from_right,
            dg,
        ]
        place = len(operands)
        return pl.pallas_call(
            tail_kernel if before is None else dropping(tail_kernel, place),
            grid=(count,),
            in_specs=[
                per_sample(rows, width, base=base),
                whole(1, width),
                square,
                square,
                square,
                square,
                per_sample(rows, width),
                per_sample(rows, width),
                per_sample(rows, 2 * width),
                per_sample(rim, 2 * width),
                per_sample(rim, 2 * width),
                per_sample(rows, width),
            ]
            + ([] if before is None else [anywhere]),
            out_specs=[
                per_sample(rows, width, base=base),
                whole(1, width),
                whole(width, 4 * width),
            ],
            out_shape=[
                shape((samples, rows, width), BF16),
                shape((1, width), F32),
                shape((width, 4 * width), F32),
            ],
            scratch_shapes=[
                pltpu.VMEM((rows, 4 * width), BF16),
                pltpu.VMEM((width, 4 * width), BF16),
            ],
            input_output_aliases={} if before is None else {place: 0},
            cost_estimate=pl.CostEstimate(
                flops=count * rows * 800000, bytes_accessed=1 << 22, transcendentals=0
            ),
            compiler_params=params,
        )(*operands, *([] if before is None else [before]))

    first = samples // 2
    cuts = [(0, first), (first, samples - first)]
    low = shifted(atoms[:, rows - rim :], "seq", 1)
    high = shifted(atoms[:, :rim], "seq", -1)
    pooled = None
    mains = []
    for base, count in cuts:
        outs = run_main(base, count, low, high, pooled)
        pooled = outs[0]
        _, gupd, dq, dkv, edge_low, edge_high, dg, gout, gtok, rsum = outs
        from_left = shifted(edge_high, "seq", 1)
        from_right = shifted(edge_low, "seq", -1)
        mains.append((gupd, dq, dkv, from_left, from_right, dg, gout, gtok, rsum))
    grad_atoms = None
    sums = []
    for (base, count), (*moved, gout, gtok, rsum) in zip(cuts, mains):
        grad_atoms, ggain, gw = run_tail(base, count, *moved, grad_atoms)
        sums.append((gout, gtok, gw, rsum, ggain))
    gq, gk, gv, gg, gout, gtok, small = sum_all(sums)
    halves = rsum.shape[1] // width
    lines = small[: halves * HEADS].reshape(halves, HEADS, width // channels, channels)
    gpair = jnp.sum(lines, axis=(0, 2)).T
    ggain = small[halves * HEADS]
    return (pooled, grad_atoms, ggain, gq, gk, gv, gg, gout, gtok, gpair)


def solution(mesh):
    placed = (
        P("samp", "seq", None),
        P(),
        P(),
        P(),
        P(),
        P(),
        P(),
        P(),
        P(),
        P("seq", None, None),
        P(),
        P("seq"),
        P("samp", "seq", None),
    )
    return jax.shard_map(
        on_device,
        mesh=mesh,
        in_specs=placed,
        out_specs=(
            P("samp", "seq", None),
            P("samp", "seq", None),
            P(),
            P(),
            P(),
            P(),
            P(),
            P(),
            P(),
            P(),
        ),
        check_vma=False,
    )
```

profile of v0, /device:TPU:0, one launch (start us, length us, event | category | flops | bytes accessed | tf_op | source)
XLA Modules:
  0.0 140.7 jit_solution(18408346198721249532)
XLA Ops:
  0.6 1.0 fusion.1
  1.7 1.3 collective-permute-start.1
  3.0 5.5 %collective-permute-start = (bf16[12,48,128]{2,1,0:T(8,128)(2,1)S(1)}, bf16[12,48,128]{2,1,0:T(8,128)(2,1)S(1)}, u32[]{:S(2)}, u32[]{:S(2)}) collective-permute-start(bf16[12,48,128]{2,1,0:T(8,128)(2,1)S(1)} %get-tuple-element.77), channel_id=1, source_target_pairs={{0,4},{4,8},{8,12},{12,16},{16,20},{20,24},{24,28},{1,5},{5,9},{9,... | collective-permute-start | bytes 442376 | tf_op jit(solution)/shard_map/ppermute | solution.py:570
  8.5 0.8 broadcast_multiply_fusion
  9.3 0.9 mul.20.wsm_ref.refs_11_
  10.2 0.2 collective-permute-done.1.high_ref.refs_3_
  10.4 3.3 %collective-permute-done.low_ref.refs_2_ = bf16[12,48,128]{2,1,0:T(8,128)(2,1)S(1)} collective-permute-done((bf16[12,48,128]{2,1,0:T(8,128)(2,1)S(1)}, bf16[12,48,128]{2,1,0:T(8,128)(2,1)S(1)}, u32[]{:S(2)}, u32[]{:S(2)}) %collective-permute-start) | collective-permute-done | bytes 147488 | tf_op jit(solution)/shard_map/ppermute | solution.py:570
  13.7 0.0 copy-done
  13.7 0.7 copy-done.1
  14.4 34.3 %shard_map.204 = (bf16[12,48,768]{2,1,0:T(8,128)(2,1)}, bf16[6,512,128]{2,1,0:T(8,128)(2,1)}, bf16[6,512,128]{2,1,0:T(8,128)(2,1)}, bf16[6,512,256]{2,1,0:T(8,12...) custom-call(s32[8]{0:T(128)} %refs_0_.2, ...), custom_call_target="tpu_custom_call" | custom-call | flops 12288000000 | bytes 4194304 | tf_op jit(solution)/shard_map/pallas_call | solution.py:643
  48.7 4.4 %collective-permute-start.4 = (bf16[6,48,256]{2,1,0:T(8,128)(2,1)}, bf16[6,48,256]{2,1,0:T(8,128)(2,1)S(1)}, u32[]{:S(2)}, u32[]{:S(2)}) collective-permute-start(bf16[6,48,256]{2,1,0:T(8,128)(2,1)} %get-tuple-element.54), channel_id=1, source_target_pairs={{0,4},{4,8},{8,12},{12,16},{16,20},{20,24},{24,28},{1,5},{5,9},{9,... | collective-permute-start | bytes 442376 | tf_op jit(solution)/shard_map/ppermute | solution.py:570
  53.1 1.5 %collective-permute-start.5 = (bf16[6,48,256]{2,1,0:T(8,128)(2,1)}, bf16[6,48,256]{2,1,0:T(8,128)(2,1)S(1)}, u32[]{:S(2)}, u32[]{:S(2)}) collective-permute-start(bf16[6,48,256]{2,1,0:T(8,128)(2,1)} %get-tuple-element.55), channel_id=1, source_target_pairs={{4,0},{8,4},{12,8},{16,12},{20,16},{24,20},{28,24},{5,1},{9,5},{13... | collective-permute-start | bytes 442376 | tf_op jit(solution)/shard_map/ppermute | solution.py:570
  54.6 34.4 %shard_map.205 = (bf16[12,48,768]{2,1,0:T(8,128)(2,1)}, bf16[6,512,128]{2,1,0:T(8,128)(2,1)}, bf16[6,512,128]{2,1,0:T(8,128)(2,1)}, bf16[6,512,256]{2,1,0:T(8,12...) custom-call(s32[8]{0:T(128)} %refs_0_.2, ...), custom_call_target="tpu_custom_call", output_to_operand_aliasing={{0}: (15, {})} | custom-call | flops 12288000000 | bytes 4194304 | tf_op jit(solution)/shard_map/pallas_call | solution.py:643
  89.0 4.6 %collective-permute-start.2 = (bf16[6,48,256]{2,1,0:T(8,128)(2,1)}, bf16[6,48,256]{2,1,0:T(8,128)(2,1)S(1)}, u32[]{:S(2)}, u32[]{:S(2)}) collective-permute-start(bf16[6,48,256]{2,1,0:T(8,128)(2,1)} %get-tuple-element.48), channel_id=1, source_target_pairs={{0,4},{4,8},{8,12},{12,16},{16,20},{20,24},{24,28},{1,5},{5,9},{9,... | collective-permute-start | bytes 442376 | tf_op jit(solution)/shard_map/ppermute | solution.py:570
  93.6 1.3 collective-permute-start.3
  94.9 0.0 collective-permute-done.4.low_ref
  94.9 0.0 collective-permute-done.5.high_ref
  94.9 0.0 copy-start.3
  94.9 0.6 copy-done.2
  95.6 0.1 copy-done.3
  95.7 7.3 %shard_map.206 = (bf16[12,512,128]{2,1,0:T(8,128)(2,1)}, f32[1,128]{1,0:T(1,128)}, f32[128,512]{1,0:T(8,128)}) custom-call(bf16[12,512,128]{2,1,0:T(8,128)(2,1)} %refs_0_.3, f32[1,128]{1,0:T(1,128)} %bitcast.17, bf16[128,128]{1,0:T(8,128)(2,1)} %refs_2_.1, bf16[128,128]{1,0:T(8,128)(2,1)} %refs_3_.1, bf16[128,128]{1,0:T(8,128)(2,1)} %refs_4_.1, ...), custom_call_target="tpu_custom_call" | custom-call | flops 2457600000 | bytes 4194304 | tf_op jit(solution)/shard_map/pallas_call | solution.py:712
  102.9 0.0 collective-permute-done.2.refs_9_
  103.0 0.0 collective-permute-done.3.refs_10_
  103.0 0.6 copy-done.4
  103.6 0.1 copy-done.5
  103.7 7.3 %shard_map.207 = (bf16[12,512,128]{2,1,0:T(8,128)(2,1)}, f32[1,128]{1,0:T(1,128)}, f32[128,512]{1,0:T(8,128)}) custom-call(bf16[12,512,128]{2,1,0:T(8,128)(2,1)} %refs_0_.3, f32[1,128]{1,0:T(1,128)} %bitcast.18, bf16[128,128]{1,0:T(8,128)(2,1)} %refs_2_.1, bf16[128,128]{1,0:T(8,128)(2,1)} %refs_3_.1, ...), custom_call_target="tpu_custom_call", output_to_operand_aliasing={{0}: (12, {})} | custom-call | flops 2457600000 | bytes 4194304 | tf_op jit(solution)/shard_map/pallas_call | solution.py:712
  111.0 25.3 %shard_map.208.packed_ref = bf16[1536,128]{1,0:T(8,128)(2,1)} custom-call(f32[128,128]{1,0:T(8,128)} %get-tuple-element.59.refs_0_, f32[128,768]{1,0:T(8,128)} %get-tuple-element.60.refs_1_, f32[128,512]{1,0:T(8,128)} %get-tuple-element.61.refs_2_, f32[64,256]{1,0:T(8,128)} %get-tuple-element.62.refs_3_, f32[1,128]{1,0:T(1,128)} %get-tuple-element.63.refs_4_, ...), custom_call_target="tpu_custom_call" | custom-call | tf_op jit(solution)/shard_map/pallas_call | solution.py:530
  136.3 1.9 %shard_map.209 = (f32[128,128]{1,0:T(8,128)}, f32[128,128]{1,0:T(8,128)}, f32[128,128]{1,0:T(8,128)}, f32[128,128]{1,0:T(8,128)}, f32[128,128]{1,0:T(8,128)}, /*index=5*/f32[128,768]{1,0:T(8,128)}, f32[16,128]{1,0:T(8,128)}) custom-call(bf16[1536,128]{1,0:T(8,128)(2,1)} %shard_map.208.packed_ref), custom_call_target="tpu_custom_call" | custom-call | tf_op jit(solution)/shard_map/pallas_call | solution.py:543
  138.2 1.2 slice_bitcast_fusion
  139.4 0.7 slice.15
  140.0 0.1 reshape.48
  140.1 0.6 reduce_sum.9
  (6 shorter events, 0.0 us)
Async XLA Ops:
  1.7 8.7 %collective-permute-start.1 = (bf16[12,48,128]{2,1,0:T(8,128)(2,1)S(1)}, bf16[12,48,128]{2,1,0:T(8,128)(2,1)S(1)}, u32[]{:S(2)}, u32[]{:S(2)}) collective-permute-start(bf16[12,48,128]{2,1,0:T(8,128)(2,1)S(1)} %get-tuple-element.76), channel_id=1, source_target_pairs={{4,0},{8,4},{12,8},{16,12},{20,16},{24,20},{28,24},{5,1},{9,5},{13... | collective-permute-start | bytes 442376 | tf_op jit(solution)/shard_map/ppermute | solution.py:570
  3.0 10.8 %collective-permute-start = (bf16[12,48,128]{2,1,0:T(8,128)(2,1)S(1)}, bf16[12,48,128]{2,1,0:T(8,128)(2,1)S(1)}, u32[]{:S(2)}, u32[]{:S(2)}) collective-permute-start(bf16[12,48,128]{2,1,0:T(8,128)(2,1)S(1)} %get-tuple-element.77), channel_id=1, source_target_pairs={{0,4},{4,8},{8,12},{12,16},{16,20},{20,24},{24,28},{1,5},{5,9},{9,... | collective-permute-start | bytes 442376 | tf_op jit(solution)/shard_map/ppermute | solution.py:570
  10.4 3.3 %copy-start = (bf16[12,48,128]{2,1,0:T(8,128)(2,1)}, bf16[12,48,128]{2,1,0:T(8,128)(2,1)S(1)}, u32[]{:S(2)}) copy-start(bf16[12,48,128]{2,1,0:T(8,128)(2,1)S(1)} %collective-permute-done.1.high_ref.refs_3_) | copy-start | bytes 442372
  13.7 0.7 copy-start.1
  48.7 46.2 %collective-permute-start.4 = (bf16[6,48,256]{2,1,0:T(8,128)(2,1)}, bf16[6,48,256]{2,1,0:T(8,128)(2,1)S(1)}, u32[]{:S(2)}, u32[]{:S(2)}) collective-permute-start(bf16[6,48,256]{2,1,0:T(8,128)(2,1)} %get-tuple-element.54), channel_id=1, source_target_pairs={{0,4},{4,8},{8,12},{12,16},{16,20},{20,24},{24,28},{1,5},{5,9},{9,... | collective-permute-start | bytes 442376 | tf_op jit(solution)/shard_map/ppermute | solution.py:570
  53.1 41.8 %collective-permute-start.5 = (bf16[6,48,256]{2,1,0:T(8,128)(2,1)}, bf16[6,48,256]{2,1,0:T(8,128)(2,1)S(1)}, u32[]{:S(2)}, u32[]{:S(2)}) collective-permute-start(bf16[6,48,256]{2,1,0:T(8,128)(2,1)} %get-tuple-element.55), channel_id=1, source_target_pairs={{4,0},{8,4},{12,8},{16,12},{20,16},{24,20},{28,24},{5,1},{9,5},{13... | collective-permute-start | bytes 442376 | tf_op jit(solution)/shard_map/ppermute | solution.py:570
  89.0 13.9 %collective-permute-start.2 = (bf16[6,48,256]{2,1,0:T(8,128)(2,1)}, bf16[6,48,256]{2,1,0:T(8,128)(2,1)S(1)}, u32[]{:S(2)}, u32[]{:S(2)}) collective-permute-start(bf16[6,48,256]{2,1,0:T(8,128)(2,1)} %get-tuple-element.48), channel_id=1, source_target_pairs={{0,4},{4,8},{8,12},{12,16},{16,20},{20,24},{24,28},{1,5},{5,9},{9,... | collective-permute-start | bytes 442376 | tf_op jit(solution)/shard_map/ppermute | solution.py:570
  93.6 9.4 %collective-permute-start.3 = (bf16[6,48,256]{2,1,0:T(8,128)(2,1)}, bf16[6,48,256]{2,1,0:T(8,128)(2,1)S(1)}, u32[]{:S(2)}, u32[]{:S(2)}) collective-permute-start(bf16[6,48,256]{2,1,0:T(8,128)(2,1)} %get-tuple-element.49), channel_id=1, source_target_pairs={{4,0},{8,4},{12,8},{16,12},{20,16},{24,20},{28,24},{5,1},{9,5},{13... | collective-permute-start | bytes 442376 | tf_op jit(solution)/shard_map/ppermute | solution.py:570
  94.9 0.7 copy-start.2
  94.9 0.7 copy-start.3
  102.9 0.7 copy-start.4
  103.0 0.7 copy-start.5
where the time goes:
time: 141 us
  Pallas kernels  111 us (79%)
  starting transfers between devices  18.5 us (13%)
  local copies, waits for them, and re-layouts  5.87 us (4%)
  waiting for transfers between devices  3.56 us (3%)
    pallas_call x2, Pallas kernels, run_main(): pl.pallas_call(main_kernel if before is None else dropping(main_kernel, p...  68.8 us
    pallas_call x1, Pallas kernels, sum_all(): pl.pallas_call(functools.partial(sum_kernel, len(halves), streams), in_sp...  25.3 us
    ppermute x6, starting transfers between devices, shifted(): return lax.ppermute(block, axis, route)  18.5 us
    pallas_call x2, Pallas kernels, run_tail(): pl.pallas_call(tail_kernel if before is None else dropping(tail_kernel, p...  14.6 us
    ppermute x6, waiting for transfers between devices, shifted(): return lax.ppermute(block, axis, route)  3.56 us
  transfers between devices with their start and end apart: 6, of which 2 were waited for; matrix products, arithmetic and copies ran while one was open for 1% of the time, Pallas kernels for 30%

commit v1 on v0

v1 whole, which is shorter than its diff:
```python
import functools

import jax
import jax.numpy as jnp
from jax import lax
from jax.experimental import pallas as pl
from jax.experimental.pallas import tpu as pltpu
from jax.sharding import PartitionSpec as P

HEADS = 4
QBLK = 32
KWIN = 128
LOG2E = 1.4426950408889634

epsilon = 1e-05
F32 = jnp.float32
BF16 = jnp.bfloat16
NN = (((1,), (0,)), ((), ()))
NT = (((1,), (1,)), ((), ()))
TN = (((0,), (0,)), ((), ()))
GROUP = 4
LANES = 128
MESH = pl.DeviceIdType.MESH


def mm(a, b, dims=NN):
    return lax.dot_general(a, b, dims, preferred_element_type=F32)


def sigmoid(x):
    return 0.5 * jnp.tanh(0.5 * x) + 0.5


def layer_norm(x, gain):
    centred = x - jnp.mean(x, axis=-1, keepdims=True)
    variance = jnp.mean(centred * centred, axis=-1, keepdims=True)
    inv_std = lax.rsqrt(variance + epsilon)
    normed = centred * inv_std
    return normed, inv_std, (normed * gain).astype(BF16)


def head_lanes(width):
    lane = lax.broadcasted_iota(jnp.int32, (1, width), 1)
    return lane // (width // HEADS)


def expand(block, masks):
    return jnp.concatenate([block * m for m in masks], axis=0)


def collapse(wide, lane_head):
    rows = wide.shape[0] // HEADS
    out = wide[:rows]
    for h in range(1, HEADS):
        out = jnp.where(lane_head == h, wide[h * rows : (h + 1) * rows], out)
    return out


def lane_swap(parts, lane_block):
    count = len(parts)
    outs = []
    for b in range(count):
        out = None
        for a in range(count):
            shift = (QBLK * (a - b)) % LANES
            moved = parts[a] if shift == 0 else pltpu.roll(parts[a], shift, 1)
            out = moved if out is None else jnp.where(lane_block == a, moved, out)
        outs.append(out)
    return outs


def pair_weights(wpair_ref, per):
    channels = wpair_ref.shape[0]
    high, wide = HEADS * per, per * channels
    row = lax.broadcasted_iota(jnp.int32, (high, HEADS), 0) // per
    head = lax.broadcasted_iota(jnp.int32, (high, HEADS), 1)
    pick = jnp.where(row == head, 1.0, 0.0).astype(BF16)
    by_row = mm(pick, wpair_ref[...], NT).astype(BF16)
    lane = lax.rem(lax.broadcasted_iota(jnp.int32, (channels, wide), 1), channels)
    chan = lax.broadcasted_iota(jnp.int32, (channels, wide), 0)
    spread = mm(by_row, jnp.where(lane == chan, 1.0, 0.0).astype(BF16))
    key = lax.rem(lax.broadcasted_iota(jnp.int32, (high, wide), 0), per)
    spot = lax.broadcasted_iota(jnp.int32, (high, wide), 1) // channels
    return jnp.where(key == spot, spread, 0.0).astype(BF16)


def build_bias(counts_ref, pair_ref, wsm, bias_scr, blocks, rows):
    pos = lax.axis_index("seq")
    size = lax.axis_size("seq")
    own = counts_ref[pos]
    left = jnp.where(pos > 0, counts_ref[jnp.maximum(pos - 1, 0)], 0)
    right = jnp.where(pos < size - 1, counts_ref[jnp.minimum(pos + 1, size - 1)], 0)
    rim = (KWIN - QBLK) // 2
    lane_block = head_lanes(LANES)
    chunk = wsm.shape[1]
    per = wsm.shape[0] // HEADS
    for kk in range(pair_ref.shape[1] // chunk):
        biased = mm(wsm, pair_ref[:, kk * chunk : (kk + 1) * chunk], NT)
        for g in range(blocks // GROUP):
            parts = [
                biased[h * per : (h + 1) * per, g * LANES : (g + 1) * LANES] for h in range(HEADS)
            ]
            for w, out in enumerate(lane_swap(parts, lane_block)):
                b = g * GROUP + w
                slot = (
                    lax.broadcasted_iota(jnp.int32, (per, LANES), 0) + kk * per + b * QBLK - rim
                )
                alive = (
                    ((slot < 0) & (slot + rows < left))
                    | ((slot >= 0) & (slot < own))
                    | ((slot >= rows) & (slot - rows < right))
                )
                bias_scr[b, kk * per : (kk + 1) * per, :] = jnp.where(alive, out * LOG2E, -1e30)


def pair_gradient(pair_ref, score_scr, per, chunk, blocks):
    lane_block = head_lanes(LANES)
    total = None
    for kk in range(pair_ref.shape[1] // chunk):
        columns = []
        for g in range(blocks // GROUP):
            parts = [score_scr[g * GROUP + w, kk * per : (kk + 1) * per, :] for w in range(GROUP)]
            columns.append(jnp.concatenate(lane_swap(parts, lane_block), axis=0))
        grads = jnp.concatenate(columns, axis=1).astype(BF16)
        part = mm(grads, pair_ref[:, kk * chunk : (kk + 1) * chunk])
        total = part if total is None else total + part
    high, wide = total.shape
    row = lax.broadcasted_iota(jnp.int32, (high, wide), 0)
    lane = lax.broadcasted_iota(jnp.int32, (high, wide), 1)
    diagonal = jnp.where(lax.rem(row, per) == lane // (wide // per), total, 0.0)
    lines = []
    for h in range(HEADS):
        line = jnp.sum(diagonal[h * per : (h + 1) * per], axis=0, keepdims=True)
        folded = line[:, :LANES]
        for n in range(1, wide // LANES):
            folded = folded + line[:, n * LANES : (n + 1) * LANES]
        lines.append(folded)
    return lines


def weave(*lists):
    lists = [x for x in lists if x]
    done = [0] * len(lists)
    while True:
        best = None
        for n, x in enumerate(lists):
            if done[n] < len(x):
                share = (done[n] + 0.5) / len(x)
                if best is None or share < best[0]:
                    best = (share, n)
        if best is None:
            return
        n = best[1]
        lists[n][done[n]]()
        done[n] += 1


def axis_sizes():
    return [(axis, lax.axis_size(axis)) for axis in ("samp", "seq")]


def shifted_index(axis, size, distance):
    return lax.rem(lax.axis_index(axis) + distance, size)


class Summer:
    def __init__(self, buf, out, streams, orders, send_sem, recv_sem, slots):
        self.buf, self.out, self.streams, self.orders = buf, out, streams, orders
        self.send_sem, self.recv_sem = send_sem, recv_sem
        self.sends, self.recvs = slots[: 2 * streams], slots[2 * streams :]
        self.unit = buf.shape[0] // streams
        self.peers = sum(size - 1 for _, size in orders[0])

    def spans(self, stream):
        (a0, s0), (a1, s1) = self.orders[stream]
        off0 = stream * self.unit
        len1 = self.unit // s0
        len2 = len1 // s1
        off1 = off0 + lax.axis_index(a0) * len1
        off2 = off1 + lax.axis_index(a1) * len2
        return [(off0, self.unit), (off1, len1), (off2, len2)]

    def copy(self, stream, src, dst, slot, partner):
        at = stream * 2 * self.peers + slot
        return pltpu.make_async_remote_copy(
            src_ref=src,
            dst_ref=dst,
            send_sem=self.send_sem.at[at],
            recv_sem=self.recv_sem.at[at],
            device_id=partner,
            device_id_type=MESH,
        )

    def scatter_copies(self, stream, k):
        axis, size = self.orders[stream][k]
        base = 0 if k == 0 else self.orders[stream][0][1] - 1
        return [
            self.copy(
                stream,
                self.sends[2 * stream + k].at[d - 1],
                self.recvs[2 * stream + k].at[d - 1],
                base + d - 1,
                {axis: shifted_index(axis, size, d)},
            )
            for d in range(1, size)
        ]

    def gather_copies(self, stream, k):
        axis, size = self.orders[stream][k]
        base = self.peers + (0 if k == 1 else self.orders[stream][1][1] - 1)
        off, length = self.spans(stream)[k + 1]
        part = self.out.at[pl.ds(pl.multiple_of(off, 16), length), :]
        return [
            self.copy(stream, part, part, base + d - 1, {axis: shifted_index(axis, size, d)})
            for d in range(1, size)
        ]

    def scatter(self, k):
        for stream in range(self.streams):
            spans = self.spans(stream)
            axis, size = self.orders[stream][k]
            if k > 0:
                off, length = spans[k]
                rows = pl.ds(pl.multiple_of(off, 16), length)
                self.buf[rows, :] = self.absorbed(stream, k - 1)
            off, length = spans[k][0], spans[k + 1][1]
            for d, copy in enumerate(self.scatter_copies(stream, k), 1):
                give = pl.multiple_of(off + shifted_index(axis, size, d) * length, 16)
                self.sends[2 * stream + k][d - 1] = self.buf[pl.ds(give, length), :].astype(BF16)
                copy.start()

    def absorbed(self, stream, k):
        off, length = self.spans(stream)[k + 1]
        value = self.buf[pl.ds(pl.multiple_of(off, 16), length), :]
        for n, copy in enumerate(self.scatter_copies(stream, k)):
            copy.wait()
            value = value + self.recvs[2 * stream + k][n].astype(F32)
        return value

    def gather(self, k):
        for stream in range(self.streams):
            if k == 1:
                off, length = self.spans(stream)[2]
                rows = pl.ds(pl.multiple_of(off, 16), length)
                self.out[rows, :] = self.absorbed(stream, 1).astype(BF16)
            else:
                for copy in self.gather_copies(stream, 1):
                    copy.wait()
            for copy in self.gather_copies(stream, k):
                copy.start()

    def finish(self):
        for stream in range(self.streams):
            for copy in self.gather_copies(stream, 0):
                copy.wait()

    def actions(self):
        return [
            lambda: self.scatter(0),
            lambda: self.scatter(1),
            lambda: self.gather(1),
            lambda: self.gather(0),
            self.finish,
        ]


def step_kernel(
    samples,
    early_streams,
    late_streams,
    counts_ref,
    atoms_hbm,
    atoms_ref,
    again_ref,
    gain_ref,
    wq_ref,
    wk_ref,
    wv_ref,
    wg_ref,
    wo_ref,
    wt_ref,
    wpair_ref,
    pair_ref,
    ids_ref,
    cot_ref,
    pooled_ref,
    gatoms_ref,
    early_ref,
    late_ref,
    small_ref,
    low_in,
    high_in,
    edge_out,
    edge_in,
    bias_scr,
    score_scr,
    member_scr,
    member_t_scr,
    inv_scr,
    wqg_scr,
    wkv_scr,
    wall_scr,
    hid_scr,
    gate_scr,
    gated_scr,
    back_scr,
    q_all,
    kv_all,
    low_all,
    gx_all,
    dg_all,
    gupd_all,
    d_scr,
    gout_scr,
    gtok_scr,
    gw_scr,
    ggain_scr,
    early_buf,
    late_buf,
    early_sum,
    late_sum,
    small_a,
    small_b,
    small_src,
    halo_send,
    halo_recv,
    edge_send,
    edge_recv,
    early_send,
    early_recv,
    late_send,
    late_recv,
    small_send,
    small_recv,
    *slots,
):
    step = pl.program_id(0)
    rows, width = q_all.shape[1:]
    blocks = rows // QBLK
    rim = (KWIN - QBLK) // 2
    tokens = inv_scr.shape[0]
    per = 2 * LANES // wpair_ref.shape[0]
    pair_chunk = per * wpair_ref.shape[0]
    scaling = (width // HEADS) ** (-0.5)
    lane_head = head_lanes(width)
    masks = [(lane_head == h).astype(F32).astype(BF16) for h in range(HEADS)]
    ones = jnp.ones((KWIN, width), BF16)
    axes = axis_sizes()
    pos = lax.axis_index("seq")
    size = lax.axis_size("seq")
    last = 2 * samples

    early_orders = [axes[::-1] if s % 2 == 1 else axes for s in range(early_streams)]
    early = Summer(
        early_buf,
        early_sum,
        early_streams,
        early_orders,
        early_send,
        early_recv,
        slots[: 4 * early_streams],
    )
    late = Summer(
        late_buf,
        late_sum,
        late_streams,
        [axes] * late_streams,
        late_send,
        late_recv,
        slots[4 * early_streams :],
    )

    def to_right(src, dst, send_sem, recv_sem):
        return pltpu.make_async_remote_copy(
            src_ref=src,
            dst_ref=dst,
            send_sem=send_sem,
            recv_sem=recv_sem,
            device_id={"seq": jnp.minimum(pos + 1, size - 1)},
            device_id_type=MESH,
        )

    def to_left(src, dst, send_sem, recv_sem):
        return pltpu.make_async_remote_copy(
            src_ref=src,
            dst_ref=dst,
            send_sem=send_sem,
            recv_sem=recv_sem,
            device_id={"seq": jnp.maximum(pos - 1, 0)},
            device_id_type=MESH,
        )

    def halo(part):
        span = pl.ds(0, 1) if part == 0 else pl.ds(1, samples - 1)
        right = to_right(
            atoms_hbm.at[span, rows - rim : rows, :],
            low_in.at[span],
            halo_send.at[0, part],
            halo_recv.at[0, part],
        )
        left = to_left(
            atoms_hbm.at[span, 0:rim, :],
            high_in.at[span],
            halo_send.at[1, part],
            halo_recv.at[1, part],
        )
        return right, left

    def edges(j):
        right = to_right(
            edge_out.at[1, j], edge_in.at[0, j], edge_send.at[0, j], edge_recv.at[0, j]
        )
        left = to_left(
            edge_out.at[0, j], edge_in.at[1, j], edge_send.at[1, j], edge_recv.at[1, j]
        )
        return right, left

    def launch(pair):
        right, left = pair

        @pl.when(pos < size - 1)
        def _():
            right.start()

        @pl.when(pos > 0)
        def _():
            left.start()

    def collect(pair):
        right, left = pair

        @pl.when(pos < size - 1)
        def _():
            right.wait_send()
            left.wait_recv()

        @pl.when(pos > 0)
        def _():
            left.wait_send()
            right.wait_recv()

    def forward_stages(s):
        slot = lax.rem(s, 2)
        gain = gain_ref[...]
        stages = []
        cuts = 4
        chunk = rows // cuts

        def rims():
            hid_scr[:rim] = layer_norm(low_in[s].astype(F32), gain)[2]
            hid_scr[rim + rows :] = layer_norm(high_in[s].astype(F32), gain)[2]
            kv_all[s, :rim] = mm(hid_scr[:rim], wkv_scr[...]).astype(BF16)
            kv_all[s, rim + rows :] = mm(hid_scr[rim + rows :], wkv_scr[...]).astype(BF16)

        def norm(c):
            def run():
                x = atoms_ref[0, c * chunk : (c + 1) * chunk].astype(F32)
                hid_scr[rim + c * chunk : rim + (c + 1) * chunk] = layer_norm(x, gain)[2]

            return run

        def project(c):
            def run():
                span = slice(c * chunk, (c + 1) * chunk)
                hidden = hid_scr[rim + c * chunk : rim + (c + 1) * chunk]
                kv_all[s, rim + c * chunk : rim + (c + 1) * chunk] = mm(
                    hidden, wkv_scr[...]
                ).astype(BF16)
                qg = mm(hidden, wqg_scr[...])
                q_all[s, span] = qg[:, :width].astype(BF16)
                gate_scr[span] = sigmoid(qg[:, width:])

            return run

        def score(spans):
            def run():
                q_exp = [expand(q_all[s, b * QBLK : (b + 1) * QBLK, :], masks) for b in spans]
                scores = [
                    mm(kv_all[s, b * QBLK : b * QBLK + KWIN, :width], q, NT)
                    for b, q in zip(spans, q_exp)
                ]
                for b, sc in zip(spans, scores):
                    low_all[s, b] = jnp.exp2(sc * (scaling * LOG2E) + bias_scr[b]).astype(BF16)

            return run

        def attend(spans):
            def run():
                wide = [
                    mm(
                        low_all[s, b],
                        jnp.concatenate(
                            [kv_all[s, b * QBLK : b * QBLK + KWIN, width:], ones], axis=1
                        ),
                        TN,
                    )
                    for b in spans
                ]
                for b, o in zip(spans, wide):
                    span = slice(b * QBLK, (b + 1) * QBLK)
                    inv = 1.0 / collapse(o[:, width:], lane_head)
                    att = collapse(o[:, :width], lane_head) * inv
                    gate = gate_scr[span]
                    gated = gate * att
                    scaled = gate * inv
                    gated_scr[slot, span] = gated.astype(BF16)
                    back_scr[slot, 0, span] = scaled
                    back_scr[slot, 1, span] = -(scaled * att)
                    back_scr[slot, 2, span] = gated * (1.0 - gate)

            return run

        stages.append(rims)
        stages.append(norm(0))
        for c in range(cuts):
            if c + 1 < cuts:
                stages.append(norm(c + 1))
            stages.append(project(c))
        groups = [
            [g * GROUP + w for w in range(GROUP)] for g in range(blocks // GROUP)
        ]
        stages.append(score(groups[0]))
        for g in range(len(groups)):
            if g + 1 < len(groups):
                stages.append(score(groups[g + 1]))
            stages.append(attend(groups[g]))
        return stages

    def token_stages(s):
        slot = lax.rem(s, 2)
        chunk = 256
        half = rows // 2
        held = {}
        stages = []

        def begin():
            gated = gated_scr[slot]
            x = again_ref[0].astype(F32)
            held["updated"] = (x + mm(gated, wo_ref[...])).astype(BF16)
            held["cot"] = (cot_ref[0].astype(F32) * inv_scr[...]).astype(BF16)
            held["gupd"] = [None, None]

        def piece(c, r):
            def run():
                cols = slice(c * chunk, (c + 1) * chunk)
                wt = wt_ref[:, cols]
                span = slice(r * half, (r + 1) * half)
                upd = held["updated"][span]
                pre = mm(upd, wt)
                sig = sigmoid(pre)
                act = pre * sig
                grad_act = mm(member_scr[span, :], held["cot"][:, cols])
                grad_pre = (grad_act * (sig + act * (1.0 - sig))).astype(BF16)
                pooled = mm(member_t_scr[:, span], act.astype(BF16))
                gtok = mm(upd, grad_pre, TN)
                part = mm(grad_pre, wt, NT)
                if r == 0:
                    held["pooled"], held["gtok"] = pooled, gtok
                else:
                    pooled_ref[0, :, cols] = ((held["pooled"] + pooled) * inv_scr[...]).astype(BF16)
                    gtok_scr[:, cols] += held["gtok"] + gtok
                before = held["gupd"][r]
                held["gupd"][r] = part if before is None else before + part

            return run

        def end():
            grad_updated = jnp.concatenate(held["gupd"], axis=0).astype(BF16)
            gupd_all[s] = grad_updated
            gout_scr[...] += mm(gated_scr[slot], grad_updated, TN)
            grad_gated = mm(grad_updated, wo_ref[...], NT)
            gx_all[s, :, :width] = (grad_gated * back_scr[slot, 0]).astype(BF16)
            gx_all[s, :, width:] = (grad_gated * back_scr[slot, 1]).astype(BF16)
            dg_all[s] = (grad_gated * back_scr[slot, 2]).astype(BF16)

        stages.append(begin)
        for c in range(wt_ref.shape[1] // chunk):
            for r in range(2):
                stages.append(piece(c, r))
        stages.append(end)
        return stages

    def backward_stages(s):
        slot = lax.rem(s, 2)
        open_k = []
        open_v = []
        held = {}
        stages = []

        def tiles(x):
            return [x[n * QBLK : (n + 1) * QBLK] for n in range(KWIN // QBLK)]

        def store(at, k, v):
            if at < rim:
                edge_out[0, s, at : at + k.shape[0], :width] = k
                edge_out[0, s, at : at + k.shape[0], width:] = v
            elif at < rim + rows:
                d_scr[slot, at - rim : at - rim + k.shape[0], width : 2 * width] = k
                d_scr[slot, at - rim : at - rim + k.shape[0], 2 * width : 3 * width] = v
            else:
                at = at - rim - rows
                edge_out[1, s, at : at + k.shape[0], :width] = k
                edge_out[1, s, at : at + k.shape[0], width:] = v

        def close(first, count):
            for n in range(count):
                at = (first + n) * QBLK
                k = (open_k[n] * scaling).astype(BF16)
                v = open_v[n].astype(BF16)
                half = QBLK // 2
                store(at, k[:half], v[:half])
                store(at + half, k[half:], v[half:])
            del open_k[:count]
            del open_v[:count]

        def merge(opened, parts):
            for n, part in enumerate(parts):
                if n < len(opened):
                    opened[n] = opened[n] + part
                else:
                    opened.append(part)

        def grads(g, spans):
            def run():
                gx = [
                    jnp.concatenate(
                        [
                            expand(gx_all[s, b * QBLK : (b + 1) * QBLK, :width], masks),
                            expand(gx_all[s, b * QBLK : (b + 1) * QBLK, width:], masks),
                        ],
                        axis=1,
                    )
                    for b in spans
                ]
                gps = [
                    mm(
                        jnp.concatenate(
                            [kv_all[s, b * QBLK : b * QBLK + KWIN, width:], ones], axis=1
                        ),
                        x,
                        NT,
                    )
                    for b, x in zip(spans, gx)
                ]
                dss = [low_all[s, b].astype(F32) * gp for b, gp in zip(spans, gps)]
                for b, ds in zip(spans, dss):
                    score_scr[b] += ds
                held[g] = [ds.astype(BF16) for ds in dss]
                held[g, "dv"] = [mm(low_all[s, b], x[:, :width]) for b, x in zip(spans, gx)]

            return run

        def products(g, spans):
            def run():
                lows = held.pop(g)
                dvs = held.pop((g, "dv"))
                q_exp = [expand(q_all[s, b * QBLK : (b + 1) * QBLK, :], masks) for b in spans]
                dks = [mm(low, q) for low, q in zip(lows, q_exp)]
                dqs = [
                    mm(low, kv_all[s, b * QBLK : b * QBLK + KWIN, :width], TN)
                    for b, low in zip(spans, lows)
                ]
                for b, dk, dv in zip(spans, dks, dvs):
                    merge(open_k, tiles(dk))
                    merge(open_v, tiles(dv))
                    close(b, 1)
                for b, dq in zip(spans, dqs):
                    d_scr[slot, b * QBLK : (b + 1) * QBLK, :width] = (
                        collapse(dq, lane_head) * scaling
                    ).astype(BF16)

            return run

        group = 2
        groups = [[g * group + w for w in range(group)] for g in range(blocks // group)]
        stages.append(grads(0, groups[0]))
        for g in range(len(groups)):
            if g + 1 < len(groups):
                stages.append(grads(g + 1, groups[g + 1]))
            stages.append(products(g, groups[g]))
        stages.append(lambda: close(blocks, len(open_k)))
        return stages

    def tail_stages(s):
        slot = lax.rem(s, 2)
        gain = gain_ref[...]
        stages = []
        cuts = 2
        chunk = rows // cuts
        held = {}

        def gather():
            d_scr[slot, :, 3 * width :] = dg_all[s]
            d_scr[slot, :rim, width : 3 * width] = (
                d_scr[slot, :rim, width : 3 * width].astype(F32) + edge_in[0, s].astype(F32)
            ).astype(BF16)
            d_scr[slot, rows - rim :, width : 3 * width] = (
                d_scr[slot, rows - rim :, width : 3 * width].astype(F32)
                + edge_in[1, s].astype(F32)
            ).astype(BF16)

        def norm(c):
            def run():
                held[c] = layer_norm(again_ref[0, c * chunk : (c + 1) * chunk].astype(F32), gain)

            return run

        def multiply(c):
            def run():
                d = d_scr[slot, c * chunk : (c + 1) * chunk]
                held["gh", c] = mm(d, wall_scr[...], NT)
                gw_scr[...] += mm(held[c][2], d, TN)

            return run

        def finish(c):
            def run():
                normed, inv_std, _ = held[c]
                grad_hidden = held["gh", c]
                gn = grad_hidden * normed
                ggain_scr[...] += jnp.sum(gn, axis=0, keepdims=True)
                gx = grad_hidden * gain
                grad_ln = inv_std * (
                    gx
                    - jnp.mean(gx, axis=-1, keepdims=True)
                    - normed * jnp.mean(gn * gain, axis=-1, keepdims=True)
                )
                span = slice(c * chunk, (c + 1) * chunk)
                gatoms_ref[0, span] = (gupd_all[s, span].astype(F32) + grad_ln).astype(BF16)

            return run

        stages.append(gather)
        for c in range(cuts):
            stages += [norm(c), multiply(c), finish(c)]
        return stages

    @pl.when(step == 0)
    def _():
        barrier = pltpu.get_barrier_semaphore()
        for axis, count in axes:
            for d in range(1, count):
                pl.semaphore_signal(
                    barrier,
                    inc=1,
                    device_id={axis: shifted_index(axis, count, d)},
                    device_id_type=MESH,
                )

        @pl.when(pos == 0)
        def _():
            low_in[...] = jnp.zeros_like(low_in)
            edge_in[0] = jnp.zeros_like(edge_in[0])

        @pl.when(pos == size - 1)
        def _():
            high_in[...] = jnp.zeros_like(high_in)
            edge_in[1] = jnp.zeros_like(edge_in[1])

        pl.semaphore_wait(barrier, sum(count - 1 for _, count in axes))
        for part in range(2):
            launch(halo(part))
        build_bias(
            counts_ref, pair_ref, pair_weights(wpair_ref, per), bias_scr, blocks, rows
        )
        token = lax.broadcasted_iota(jnp.int32, (tokens, rows), 0)
        place = lax.broadcasted_iota(jnp.int32, (tokens, rows), 1)
        hit = (ids_ref[...] - pos * tokens == token) & (place < counts_ref[pos])
        member_t = jnp.where(hit, 1.0, 0.0).astype(F32)
        inv_scr[...] = 1.0 / jnp.sum(member_t, axis=1, keepdims=True)
        member_t_scr[...] = member_t.astype(BF16)
        member_scr[...] = member_t.T.astype(BF16)
        wqg_scr[:, :width] = wq_ref[...]
        wqg_scr[:, width:] = wg_ref[...]
        wkv_scr[:, :width] = wk_ref[...]
        wkv_scr[:, width:] = wv_ref[...]
        for n, ref in enumerate((wq_ref, wk_ref, wv_ref, wg_ref)):
            wall_scr[:, n * width : (n + 1) * width] = ref[...]
        for ref in (score_scr, gout_scr, gtok_scr, gw_scr, ggain_scr):
            ref[...] = jnp.zeros_like(ref)
        collect(halo(0))
        weave(forward_stages(0))
        collect(halo(1))

    @pl.when((step > 0) & (step < samples))
    def _():
        weave(token_stages(step - 1), forward_stages(step))

    @pl.when(step == samples)
    def _():
        weave(token_stages(samples - 1), backward_stages(0))

    @pl.when((step > samples) & (step < last))
    def _():
        collect(edges(step - samples - 1))
        weave(tail_stages(step - samples - 1), backward_stages(step - samples))

    @pl.when((step >= samples) & (step < last))
    def _():
        launch(edges(step - samples))

    def fill_early():
        for n in range(gtok_scr.shape[1] // width):
            early_buf[n * width : (n + 1) * width, :] = gtok_scr[:, n * width : (n + 1) * width]
        at = gtok_scr.shape[1]
        early_buf[at : at + width, :] = gout_scr[...]
        early_buf[at + width :, :] = jnp.zeros((early_buf.shape[0] - at - width, width), F32)

    for n, action in enumerate(early.actions()):

        def run(n=n, action=action):
            if n == 0:
                fill_early()
            action()

        pl.when(step == min(samples + 2 * n, last))(run)

    @pl.when(step == last)
    def _():
        lines = pair_gradient(pair_ref, score_scr, per, pair_chunk, blocks)
        collect(edges(samples - 1))
        weave(tail_stages(samples - 1))
        for n in range(4):
            late_buf[n * width : (n + 1) * width, :] = gw_scr[:, n * width : (n + 1) * width]
        if late_buf.shape[0] > 4 * width:
            late_buf[4 * width :, :] = jnp.zeros((late_buf.shape[0] - 4 * width, width), F32)
        acts = late.actions()
        acts[0]()
        small_src[0] = jnp.concatenate(
            lines + [ggain_scr[...], jnp.zeros((8 - HEADS - 1, width), F32)], axis=0
        )

        def small_copies(k):
            axis, count = axes[k]
            base = 0 if k == 0 else axes[0][1] - 1
            return [
                pltpu.make_async_remote_copy(
                    src_ref=small_src.at[k],
                    dst_ref=(small_a, small_b)[k].at[d - 1],
                    send_sem=small_send.at[base + d - 1],
                    recv_sem=small_recv.at[base + d - 1],
                    device_id={axis: shifted_index(axis, count, d)},
                    device_id_type=MESH,
                )
                for d in range(1, count)
            ]

        for copy in small_copies(0):
            copy.start()
        acts[1]()
        value = small_src[0]
        for n, copy in enumerate(small_copies(0)):
            copy.wait()
            value = value + small_a[n]
        small_src[1] = value
        for copy in small_copies(1):
            copy.start()
        acts[2]()
        for n, copy in enumerate(small_copies(1)):
            copy.wait()
            value = value + small_b[n]
        small_ref[...] = value
        acts[3]()
        early_ref[...] = early_sum[...]
        acts[4]()
        late_ref[...] = late_sum[...]


def unpack_kernel(
    channels,
    early_ref,
    late_ref,
    small_ref,
    ggain_out,
    gq_out,
    gk_out,
    gv_out,
    gg_out,
    gout_out,
    gtok_out,
    gpair_out,
):
    width = gout_out.shape[0]
    blocks = gtok_out.shape[1] // width

    def block(ref, n):
        return ref[n * width : (n + 1) * width, :].astype(F32)

    for n in range(blocks):
        gtok_out[:, n * width : (n + 1) * width] = block(early_ref, n)
    gout_out[...] = block(early_ref, blocks)
    for n, ref in enumerate((gq_out, gk_out, gv_out, gg_out)):
        ref[...] = block(late_ref, n)
    lines = small_ref[...]
    ggain_out[...] = lines[HEADS : HEADS + 1]
    shift = width // 2
    while shift >= channels:
        lines = lines + pltpu.roll(lines, shift, 1)
        shift //= 2
    gpair_out[...] = lines[:HEADS, :channels]


def whole(*shape):
    return pl.BlockSpec(shape, lambda s: (0,) * len(shape))


def sum_scratch(total, streams, orders, width):
    unit = total // streams
    slots = []
    for stream in range(streams):
        length = unit
        for _, size in orders[stream]:
            length //= size
            slots.append(pltpu.VMEM((size - 1, length, width), BF16))
    return slots * 2


def on_device(
    atoms,
    gain,
    w_query,
    w_key,
    w_value,
    w_gate,
    w_out,
    w_token,
    w_pair,
    pair_cond,
    counts,
    membership,
    pooled_cot,
):
    samples, rows, width = atoms.shape
    blocks = rows // QBLK
    rim = (KWIN - QBLK) // 2
    tokens, token_width = pooled_cot.shape[1:]
    channels = w_pair.shape[0]
    pair2 = pair_cond.reshape(blocks * QBLK, pair_cond.shape[-1])
    gain2 = gain.reshape(1, width)
    ids2 = membership.reshape(1, rows)
    square = whole(width, width)
    shape = jax.ShapeDtypeStruct
    vmem = pltpu.VMEM
    dma = pltpu.SemaphoreType.DMA

    axes = axis_sizes()
    devices = axes[0][1] * axes[1][1]
    peers = sum(size - 1 for _, size in axes)
    unit = 16 * devices
    early_total = -(-(token_width + width) // unit) * unit
    late_total = -(-(4 * width) // unit) * unit
    early_streams = early_total // unit
    late_streams = late_total // unit
    early_orders = [axes[::-1] if s % 2 == 1 else axes for s in range(early_streams)]

    def clip(x):
        return jnp.clip(x, 0, samples - 1)

    def again(i):
        return jnp.where(i <= samples, clip(i - 1), clip(i - samples - 1))

    pooled, gatoms, early, late, small = pl.pallas_call(
        functools.partial(step_kernel, samples, early_streams, late_streams),
        grid=(2 * samples + 1,),
        in_specs=[
            pl.BlockSpec(memory_space=pltpu.SMEM),
            pl.BlockSpec(memory_space=pl.ANY),
            pl.BlockSpec((1, rows, width), lambda i: (clip(i), 0, 0)),
            pl.BlockSpec((1, rows, width), lambda i: (again(i), 0, 0)),
            whole(1, width),
            square,
            square,
            square,
            square,
            square,
            whole(width, token_width),
            whole(*w_pair.shape),
            whole(*pair2.shape),
            whole(1, rows),
            pl.BlockSpec((1, tokens, token_width), lambda i: (clip(i - 1), 0, 0)),
        ],
        out_specs=[
            pl.BlockSpec((1, tokens, token_width), lambda i: (clip(i - 1), 0, 0)),
            pl.BlockSpec((1, rows, width), lambda i: (clip(i - samples - 1), 0, 0)),
            whole(early_total, width),
            whole(late_total, width),
            whole(8, width),
        ],
        out_shape=[
            shape((samples, tokens, token_width), BF16),
            shape((samples, rows, width), BF16),
            shape((early_total, width), BF16),
            shape((late_total, width), BF16),
            shape((8, width), F32),
        ],
        scratch_shapes=[
            vmem((samples, rim, width), BF16),
            vmem((samples, rim, width), BF16),
            vmem((2, samples, rim, 2 * width), BF16),
            vmem((2, samples, rim, 2 * width), BF16),
            vmem((blocks, KWIN, LANES), F32),
            vmem((blocks, KWIN, LANES), F32),
            vmem((rows, tokens), BF16),
            vmem((tokens, rows), BF16),
            vmem((tokens, 1), F32),
            vmem((width, 2 * width), BF16),
            vmem((width, 2 * width), BF16),
            vmem((width, 4 * width), BF16),
            vmem((rows + 2 * rim, width), BF16),
            vmem((rows, width), F32),
            vmem((2, rows, width), BF16),
            vmem((2, 3, rows, width), F32),
            vmem((samples, rows, width), BF16),
            vmem((samples, rows + 2 * rim, 2 * width), BF16),
            vmem((samples, blocks, KWIN, LANES), BF16),
            vmem((samples, rows, 2 * width), BF16),
            vmem((samples, rows, width), BF16),
            vmem((samples, rows, width), BF16),
            vmem((2, rows, 4 * width), BF16),
            vmem((width, width), F32),
            vmem((width, token_width), F32),
            vmem((width, 4 * width), F32),
            vmem((1, width), F32),
            vmem((early_total, width), F32),
            vmem((late_total, width), F32),
            vmem((early_total, width), BF16),
            vmem((late_total, width), BF16),
            vmem((axes[0][1] - 1, 8, width), F32),
            vmem((axes[1][1] - 1, 8, width), F32),
            vmem((2, 8, width), F32),
            dma((2, 2)),
            dma((2, 2)),
            dma((2, samples)),
            dma((2, samples)),
            dma((2 * early_streams * peers,)),
            dma((2 * early_streams * peers,)),
            dma((2 * late_streams * peers,)),
            dma((2 * late_streams * peers,)),
            dma((peers,)),
            dma((peers,)),
        ]
        + sum_scratch(early_total, early_streams, early_orders, width)
        + sum_scratch(late_total, late_streams, [axes] * late_streams, width),
        compiler_params=pltpu.CompilerParams(
            dimension_semantics=("arbitrary",),
            vmem_limit_bytes=56 * 1024 * 1024,
            collective_id=0,
            has_side_effects=True,
        ),
    )(
        counts,
        atoms,
        atoms,
        atoms,
        gain2,
        w_query,
        w_key,
        w_value,
        w_gate,
        w_out,
        w_token,
        w_pair,
        pair2,
        ids2,
        pooled_cot,
    )
    spec = pl.BlockSpec(memory_space=pltpu.VMEM)
    ggain, gq, gk, gv, gg, gout, gtok, gpair = pl.pallas_call(
        functools.partial(unpack_kernel, channels),
        in_specs=[spec] * 3,
        out_specs=[spec] * 8,
        out_shape=[shape((1, width), F32)]
        + [shape((width, width), F32)] * 5
        + [shape((width, token_width), F32), shape((HEADS, channels), F32)],
    )(early, late, small)
    return (pooled, gatoms, ggain.reshape(width), gq, gk, gv, gg, gout, gtok, gpair.T)


def solution(mesh):
    placed = (
        P("samp", "seq", None),
        P(),
        P(),
        P(),
        P(),
        P(),
        P(),
        P(),
        P(),
        P("seq", None, None),
        P(),
        P("seq"),
        P("samp", "seq", None),
    )
    return jax.shard_map(
        on_device,
        mesh=mesh,
        in_specs=placed,
        out_specs=(
            P("samp", "seq", None),
            P("samp", "seq", None),
            P(),
            P(),
            P(),
            P(),
            P(),
            P(),
            P(),
            P(),
        ),
        check_vma=False,
    )
```

time: 141 us -> 137 us (0.972)
  Pallas kernels: 111 us -> 132 us
  starting transfers between devices: 18.5 us -> 0 us
  waiting for transfers between devices: 3.56 us -> 0 us
    pallas_call x6 -> x2, Pallas kernels: 111 us -> 132 us  [the longest x1 130 us: on_device(): pl.pallas_call(functools.partial(step_kernel, samples, early_streams, lat...]
    ppermute x6 -> x0, starting transfers between devices: 18.5 us -> none  [shifted(): return lax.ppermute(block, axis, route)]
    ppermute x6 -> x0, waiting for transfers between devices: 3.56 us -> none  [shifted(): return lax.ppermute(block, axis, route)]
    unnamed x12 -> x5, local copies, waits for them, and re-layouts: 2.09 us -> 4.64 us
    slice x2 -> x0, local copies, waits for them, and re-layouts: 1.67 us -> none  [the longest x1 1.01 us: on_device(): high = shifted(atoms[:, :rim], 'seq', -1)]
  transfers between devices with their start and end apart: 6 -> 0, of which waited for: 2 -> 0; matrix products, arithmetic and copies ran while one was open for 1% -> 0% of each run, Pallas kernels for 30% -> 0%
where the time goes in v1:
time: 137 us
  Pallas kernels  132 us (96%)
  local copies, waits for them, and re-layouts  4.64 us (3%)
    pallas_call x1, Pallas kernels, on_device(): pl.pallas_call(functools.partial(step_kernel, samples, early_streams, lat...  130 us
    unnamed x5, local copies, waits for them, and re-layouts  4.64 us

profile of v1, /device:TPU:0, one launch (start us, length us, event | category | flops | bytes accessed | tf_op | source)
XLA Modules:
  0.0 136.9 jit_solution(16538322332032531316)
XLA Ops:
  0.6 1.4 copy.23.wpair_ref
  2.0 129.5 %shard_map.204 = (bf16[12,48,768]{2,1,0:T(8,128)(2,1)}, bf16[12,512,128]{2,1,0:T(8,128)(2,1)}, bf16[1024,128]{1,0:T(8,128)(2,1)}, bf16[512,128]{1,0:T(8,128)(2,1)}, f32[8,128]{1,0:T(8,128)}) custom-call(s32[8]{0:T(128)} %counts_ref.1, bf16[12,512,128]{2,1,0:T(8,128)(2,1)} %again_ref.1, bf16[12,512,128]{2,1,0:T(8,128)(2,1)} %again_ref.1, ...), custom_call_target="tpu_custom_call" | custom-call | tf_op jit(solution)/shard_map/pallas_call | solution.py:962
  131.5 0.0 copy-start
  131.5 2.1 %shard_map.205 = (f32[1,128]{1,0:T(1,128)}, f32[128,128]{1,0:T(8,128)}, f32[128,128]{1,0:T(8,128)}, f32[128,128]{1,0:T(8,128)}, f32[128,128]{1,0:T(8,128)}, /*in...) custom-call(bf16[1024,128]{1,0:T(8,128)(2,1)} %get-tuple-element.25.early_ref, ...), custom_call_target="tpu_custom_call" | custom-call | tf_op jit(solution)/shard_map/pallas_call | solution.py:1068
  133.6 2.1 %copy.26 = bf16[12,48,768]{2,1,0:T(8,128)(2,1)} copy(bf16[12,48,768]{2,1,0:T(8,128)(2,1)} %get-tuple-element.46) | data formatting | bytes 1769472
  135.7 0.0 copy-done
  135.7 1.1 copy.27
Async XLA Ops:
  131.5 4.2 %copy-start = (bf16[12,512,128]{2,1,0:T(8,128)(2,1)S(1)}, bf16[12,512,128]{2,1,0:T(8,128)(2,1)}, u32[]{:S(2)}) copy-start(bf16[12,512,128]{2,1,0:T(8,128)(2,1)} %get-tuple-element.47) | copy-start | bytes 4718596

commit v2 on v1

--- a/solution.py
+++ b/solution.py
@@ -19,8 +19,11 @@
 NT = (((1,), (1,)), ((), ()))
 TN = (((0,), (0,)), ((), ()))
 GROUP = 4
+FGROUP = 4
+PARTS = 2
 LANES = 128
 MESH = pl.DeviceIdType.MESH
+LAG = 3
 
 
 def mm(a, b, dims=NN):
@@ -70,12 +73,12 @@
 
 
 def pair_weights(wpair_ref, per):
-    channels = wpair_ref.shape[0]
+    channels = wpair_ref.shape[1]
     high, wide = HEADS * per, per * channels
     row = lax.broadcasted_iota(jnp.int32, (high, HEADS), 0) // per
     head = lax.broadcasted_iota(jnp.int32, (high, HEADS), 1)
     pick = jnp.where(row == head, 1.0, 0.0).astype(BF16)
-    by_row = mm(pick, wpair_ref[...], NT).astype(BF16)
+    by_row = mm(pick, wpair_ref[...]).astype(BF16)
     lane = lax.rem(lax.broadcasted_iota(jnp.int32, (channels, wide), 1), channels)
     chan = lax.broadcasted_iota(jnp.int32, (channels, wide), 0)
     spread = mm(by_row, jnp.where(lane == chan, 1.0, 0.0).astype(BF16))
@@ -300,21 +303,19 @@
     wqg_scr,
     wkv_scr,
     wall_scr,
-    hid_scr,
+    hid_all,
     gate_scr,
     gated_scr,
     back_scr,
     q_all,
     kv_all,
     low_all,
-    gx_all,
-    dg_all,
+    gatt_all,
     gupd_all,
-    d_scr,
+    d_all,
     gout_scr,
     gtok_scr,
     gw_scr,
-    ggain_scr,
     early_buf,
     late_buf,
     early_sum,
@@ -339,16 +340,15 @@
     blocks = rows // QBLK
     rim = (KWIN - QBLK) // 2
     tokens = inv_scr.shape[0]
-    per = 2 * LANES // wpair_ref.shape[0]
-    pair_chunk = per * wpair_ref.shape[0]
+    per = 2 * LANES // wpair_ref.shape[1]
+    pair_chunk = per * wpair_ref.shape[1]
     scaling = (width // HEADS) ** (-0.5)
     lane_head = head_lanes(width)
     masks = [(lane_head == h).astype(F32).astype(BF16) for h in range(HEADS)]
-    ones = jnp.ones((KWIN, width), BF16)
     axes = axis_sizes()
     pos = lax.axis_index("seq")
     size = lax.axis_size("seq")
-    last = 2 * samples
+    last = 3 * samples - 1
 
     early_orders = [axes[::-1] if s % 2 == 1 else axes for s in range(early_streams)]
     early = Summer(
@@ -443,26 +443,27 @@
         slot = lax.rem(s, 2)
         gain = gain_ref[...]
         stages = []
+        held = {}
         cuts = 4
         chunk = rows // cuts
 
         def rims():
-            hid_scr[:rim] = layer_norm(low_in[s].astype(F32), gain)[2]
-            hid_scr[rim + rows :] = layer_norm(high_in[s].astype(F32), gain)[2]
-            kv_all[s, :rim] = mm(hid_scr[:rim], wkv_scr[...]).astype(BF16)
-            kv_all[s, rim + rows :] = mm(hid_scr[rim + rows :], wkv_scr[...]).astype(BF16)
+            hid_all[s, :rim] = layer_norm(low_in[s].astype(F32), gain)[2]
+            hid_all[s, rim + rows :] = layer_norm(high_in[s].astype(F32), gain)[2]
+            kv_all[s, :rim] = mm(hid_all[s, :rim], wkv_scr[...]).astype(BF16)
+            kv_all[s, rim + rows :] = mm(hid_all[s, rim + rows :], wkv_scr[...]).astype(BF16)
 
         def norm(c):
             def run():
                 x = atoms_ref[0, c * chunk : (c + 1) * chunk].astype(F32)
-                hid_scr[rim + c * chunk : rim + (c + 1) * chunk] = layer_norm(x, gain)[2]
+                hid_all[s, rim + c * chunk : rim + (c + 1) * chunk] = layer_norm(x, gain)[2]
 
             return run
 
         def project(c):
             def run():
                 span = slice(c * chunk, (c + 1) * chunk)
-                hidden = hid_scr[rim + c * chunk : rim + (c + 1) * chunk]
+                hidden = hid_all[s, rim + c * chunk : rim + (c + 1) * chunk]
                 kv_all[s, rim + c * chunk : rim + (c + 1) * chunk] = mm(
                     hidden, wkv_scr[...]
                 ).astype(BF16)
@@ -472,41 +473,42 @@
 
             return run
 
-        def score(spans):
+        def score(g, spans):
             def run():
                 q_exp = [expand(q_all[s, b * QBLK : (b + 1) * QBLK, :], masks) for b in spans]
-                scores = [
+                held[g] = [
                     mm(kv_all[s, b * QBLK : b * QBLK + KWIN, :width], q, NT)
                     for b, q in zip(spans, q_exp)
                 ]
-                for b, sc in zip(spans, scores):
-                    low_all[s, b] = jnp.exp2(sc * (scaling * LOG2E) + bias_scr[b]).astype(BF16)
+
+            return run
+
+        def soften(g, spans):
+            def run():
+                es = [
+                    jnp.exp2(sc * (scaling * LOG2E) + bias_scr[b])
+                    for b, sc in zip(spans, held.pop(g))
+                ]
+                invs = [1.0 / jnp.sum(e, axis=0, keepdims=True) for e in es]
+                for b, e, inv in zip(spans, es, invs):
+                    low_all[s, b] = (e * inv).astype(BF16)
 
             return run
 
         def attend(spans):
             def run():
                 wide = [
-                    mm(
-                        low_all[s, b],
-                        jnp.concatenate(
-                            [kv_all[s, b * QBLK : b * QBLK + KWIN, width:], ones], axis=1
-                        ),
-                        TN,
-                    )
+                    mm(low_all[s, b], kv_all[s, b * QBLK : b * QBLK + KWIN, width:], TN)
                     for b in spans
                 ]
                 for b, o in zip(spans, wide):
                     span = slice(b * QBLK, (b + 1) * QBLK)
-                    inv = 1.0 / collapse(o[:, width:], lane_head)
-                    att = collapse(o[:, :width], lane_head) * inv
+                    att = collapse(o, lane_head)
                     gate = gate_scr[span]
                     gated = gate * att
-                    scaled = gate * inv
                     gated_scr[slot, span] = gated.astype(BF16)
-                    back_scr[slot, 0, span] = scaled
-                    back_scr[slot, 1, span] = -(scaled * att)
-                    back_scr[slot, 2, span] = gated * (1.0 - gate)
+                    back_scr[slot, 0, span] = gate
+                    back_scr[slot, 1, span] = gated * (1.0 - gate)
 
             return run
 
@@ -516,14 +518,15 @@
             if c + 1 < cuts:
                 stages.append(norm(c + 1))
             stages.append(project(c))
-        groups = [
-            [g * GROUP + w for w in range(GROUP)] for g in range(blocks // GROUP)
-        ]
-        stages.append(score(groups[0]))
-        for g in range(len(groups)):
-            if g + 1 < len(groups):
-                stages.append(score(groups[g + 1]))
-            stages.append(attend(groups[g]))
+        groups = [[g * FGROUP + w for w in range(FGROUP)] for g in range(blocks // FGROUP)]
+        count = len(groups)
+        for g in range(count + 2):
+            if g < count:
+                stages.append(score(g, groups[g]))
+            if 0 <= g - 1 < count:
+                stages.append(soften(g - 1, groups[g - 1]))
+            if 0 <= g - 2 < count:
+                stages.append(attend(groups[g - 2]))
         return stages
 
     def token_stages(s):
@@ -540,20 +543,40 @@
             held["cot"] = (cot_ref[0].astype(F32) * inv_scr[...]).astype(BF16)
             held["gupd"] = [None, None]
 
-        def piece(c, r):
+        def enter(c, r):
             def run():
                 cols = slice(c * chunk, (c + 1) * chunk)
-                wt = wt_ref[:, cols]
                 span = slice(r * half, (r + 1) * half)
-                upd = held["updated"][span]
-                pre = mm(upd, wt)
+                held[c, r] = (
+                    mm(held["updated"][span], wt_ref[:, cols]),
+                    mm(member_scr[span, :], held["cot"][:, cols]),
+                    [],
+                    [],
+                )
+
+            return run
+
+        def act(c, r, n):
+            def run():
+                pre, grad_act, acts, grads = held[c, r]
+                part = slice(n * half // PARTS, (n + 1) * half // PARTS)
+                pre, grad_act = pre[part], grad_act[part]
                 sig = sigmoid(pre)
-                act = pre * sig
-                grad_act = mm(member_scr[span, :], held["cot"][:, cols])
-                grad_pre = (grad_act * (sig + act * (1.0 - sig))).astype(BF16)
-                pooled = mm(member_t_scr[:, span], act.astype(BF16))
-                gtok = mm(upd, grad_pre, TN)
-                part = mm(grad_pre, wt, NT)
+                value = pre * sig
+                acts.append(value.astype(BF16))
+                grads.append((grad_act * (sig + value * (1.0 - sig))).astype(BF16))
+
+            return run
+
+        def leave(c, r):
+            def run():
+                _, _, acts, grads = held.pop((c, r))
+                cols = slice(c * chunk, (c + 1) * chunk)
+                span = slice(r * half, (r + 1) * half)
+                grad_pre = jnp.concatenate(grads, axis=0)
+                pooled = mm(member_t_scr[:, span], jnp.concatenate(acts, axis=0))
+                gtok = mm(held["updated"][span], grad_pre, TN)
+                part = mm(grad_pre, wt_ref[:, cols], NT)
                 if r == 0:
                     held["pooled"], held["gtok"] = pooled, gtok
                 else:
@@ -569,19 +592,22 @@
             gupd_all[s] = grad_updated
             gout_scr[...] += mm(gated_scr[slot], grad_updated, TN)
             grad_gated = mm(grad_updated, wo_ref[...], NT)
-            gx_all[s, :, :width] = (grad_gated * back_scr[slot, 0]).astype(BF16)
-            gx_all[s, :, width:] = (grad_gated * back_scr[slot, 1]).astype(BF16)
-            dg_all[s] = (grad_gated * back_scr[slot, 2]).astype(BF16)
+            gatt_all[s] = (grad_gated * back_scr[slot, 0]).astype(BF16)
+            d_all[s, :, 3 * width :] = (grad_gated * back_scr[slot, 1]).astype(BF16)
 
         stages.append(begin)
-        for c in range(wt_ref.shape[1] // chunk):
-            for r in range(2):
-                stages.append(piece(c, r))
+        pieces = [(c, r) for c in range(wt_ref.shape[1] // chunk) for r in range(2)]
+        for n in range(len(pieces) + 1):
+            if n < len(pieces):
+                stages.append(enter(*pieces[n]))
+            if n > 0:
+                for part in range(PARTS):
+                    stages.append(act(*pieces[n - 1], part))
+                stages.append(leave(*pieces[n - 1]))
         stages.append(end)
         return stages
 
     def backward_stages(s):
-        slot = lax.rem(s, 2)
         open_k = []
         open_v = []
         held = {}
@@ -595,8 +621,8 @@
                 edge_out[0, s, at : at + k.shape[0], :width] = k
                 edge_out[0, s, at : at + k.shape[0], width:] = v
             elif at < rim + rows:
-                d_scr[slot, at - rim : at - rim + k.shape[0], width : 2 * width] = k
-                d_scr[slot, at - rim : at - rim + k.shape[0], 2 * width : 3 * width] = v
+                d_all[s, at - rim : at - rim + k.shape[0], width : 2 * width] = k
+                d_all[s, at - rim : at - rim + k.shape[0], 2 * width : 3 * width] = v
             else:
                 at = at - rim - rows
                 edge_out[1, s, at : at + k.shape[0], :width] = k
@@ -622,31 +648,19 @@
 
         def grads(g, spans):
             def run():
-                gx = [
-                    jnp.concatenate(
-                        [
-                            expand(gx_all[s, b * QBLK : (b + 1) * QBLK, :width], masks),
-                            expand(gx_all[s, b * QBLK : (b + 1) * QBLK, width:], masks),
-                        ],
-                        axis=1,
-                    )
-                    for b in spans
+                ges = [expand(gatt_all[s, b * QBLK : (b + 1) * QBLK, :], masks) for b in spans]
+                gps = [
+                    mm(kv_all[s, b * QBLK : b * QBLK + KWIN, width:], ge, NT)
+                    for b, ge in zip(spans, ges)
                 ]
-                gps = [
-                    mm(
-                        jnp.concatenate(
-                            [kv_all[s, b * QBLK : b * QBLK + KWIN, width:], ones], axis=1
-                        ),
-                        x,
-                        NT,
-                    )
-                    for b, x in zip(spans, gx)
-                ]
-                dss = [low_all[s, b].astype(F32) * gp for b, gp in zip(spans, gps)]
+                ps = [low_all[s, b].astype(F32) for b in spans]
+                ts = [p * gp for p, gp in zip(ps, gps)]
+                sums = [jnp.sum(t, axis=0, keepdims=True) for t in ts]
+                dss = [t - p * total for p, t, total in zip(ps, ts, sums)]
                 for b, ds in zip(spans, dss):
                     score_scr[b] += ds
                 held[g] = [ds.astype(BF16) for ds in dss]
-                held[g, "dv"] = [mm(low_all[s, b], x[:, :width]) for b, x in zip(spans, gx)]
+                held[g, "dv"] = [mm(low_all[s, b], ge) for b, ge in zip(spans, ges)]
 
             return run
 
@@ -665,7 +679,7 @@
                     merge(open_v, tiles(dv))
                     close(b, 1)
                 for b, dq in zip(spans, dqs):
-                    d_scr[slot, b * QBLK : (b + 1) * QBLK, :width] = (
+                    d_all[s, b * QBLK : (b + 1) * QBLK, :width] = (
                         collapse(dq, lane_head) * scaling
                     ).astype(BF16)
 
@@ -681,24 +695,33 @@
         stages.append(lambda: close(blocks, len(open_k)))
         return stages
 
-    def tail_stages(s):
-        slot = lax.rem(s, 2)
+    def weight_stages(s):
+        cuts = 2
+        chunk = rows // cuts
+
+        def join():
+            for side, at in ((0, 0), (1, rows - rim)):
+                d_all[s, at : at + rim, width : 3 * width] = (
+                    d_all[s, at : at + rim, width : 3 * width].astype(F32)
+                    + edge_in[side, s].astype(F32)
+                ).astype(BF16)
+
+        def multiply(c):
+            def run():
+                hidden = hid_all[s, rim + c * chunk : rim + (c + 1) * chunk]
+                gw_scr[...] += mm(hidden, d_all[s, c * chunk : (c + 1) * chunk], TN)
+
+            return run
+
+        return [join] + [multiply(c) for c in range(cuts)]
+
+    def finish_stages(s):
         gain = gain_ref[...]
         stages = []
         cuts = 2
         chunk = rows // cuts
         held = {}
 
-        def gather():
-            d_scr[slot, :, 3 * width :] = dg_all[s]
-            d_scr[slot, :rim, width : 3 * width] = (
-                d_scr[slot, :rim, width : 3 * width].astype(F32) + edge_in[0, s].astype(F32)
-            ).astype(BF16)
-            d_scr[slot, rows - rim :, width : 3 * width] = (
-                d_scr[slot, rows - rim :, width : 3 * width].astype(F32)
-                + edge_in[1, s].astype(F32)
-            ).astype(BF16)
-
         def norm(c):
             def run():
                 held[c] = layer_norm(again_ref[0, c * chunk : (c + 1) * chunk].astype(F32), gain)
@@ -707,32 +730,28 @@
 
         def multiply(c):
             def run():
-                d = d_scr[slot, c * chunk : (c + 1) * chunk]
-                held["gh", c] = mm(d, wall_scr[...], NT)
-                gw_scr[...] += mm(held[c][2], d, TN)
+                held["gh", c] = mm(d_all[s, c * chunk : (c + 1) * chunk], wall_scr[...], NT)
 
             return run
 
         def finish(c):
             def run():
                 normed, inv_std, _ = held[c]
-                grad_hidden = held["gh", c]
-                gn = grad_hidden * normed
-                ggain_scr[...] += jnp.sum(gn, axis=0, keepdims=True)
-                gx = grad_hidden * gain
+                gx = held["gh", c] * gain
                 grad_ln = inv_std * (
                     gx
                     - jnp.mean(gx, axis=-1, keepdims=True)
-                    - normed * jnp.mean(gn * gain, axis=-1, keepdims=True)
+                    - normed * jnp.mean(gx * normed, axis=-1, keepdims=True)
                 )
                 span = slice(c * chunk, (c + 1) * chunk)
                 gatoms_ref[0, span] = (gupd_all[s, span].astype(F32) + grad_ln).astype(BF16)
 
             return run
 
-        stages.append(gather)
         for c in range(cuts):
-            stages += [norm(c), multiply(c), finish(c)]
+            stages += [norm(c), multiply(c)]
+        for c in range(cuts):
+            stages.append(finish(c))
         return stages
 
     @pl.when(step == 0)
@@ -776,7 +795,7 @@
         wkv_scr[:, width:] = wv_ref[...]
         for n, ref in enumerate((wq_ref, wk_ref, wv_ref, wg_ref)):
             wall_scr[:, n * width : (n + 1) * width] = ref[...]
-        for ref in (score_scr, gout_scr, gtok_scr, gw_scr, ggain_scr):
+        for ref in (score_scr, gout_scr, gtok_scr, gw_scr):
             ref[...] = jnp.zeros_like(ref)
         collect(halo(0))
         weave(forward_stages(0))
@@ -790,14 +809,29 @@
     def _():
         weave(token_stages(samples - 1), backward_stages(0))
 
-    @pl.when((step > samples) & (step < last))
+    @pl.when((step > samples) & (step < samples + LAG))
     def _():
-        collect(edges(step - samples - 1))
-        weave(tail_stages(step - samples - 1), backward_stages(step - samples))
-
-    @pl.when((step >= samples) & (step < last))
+        weave(backward_stages(step - samples))
+
+    @pl.when((step >= samples + LAG) & (step < 2 * samples))
+    def _():
+        collect(edges(step - samples - LAG))
+        weave(weight_stages(step - samples - LAG), backward_stages(step - samples))
+
+    @pl.when((step >= samples) & (step < 2 * samples))
     def _():
         launch(edges(step - samples))
+
+    @pl.when(step >= 2 * samples)
+    def _():
+        weave(finish_stages(step - 2 * samples))
+
+    @pl.when(step == 2 * samples)
+    def _():
+        lines = pair_gradient(pair_ref, score_scr, per, pair_chunk, blocks)
+        for n, line in enumerate(lines):
+            small_src[0, n : n + 1, :] = line
+        small_src[0, HEADS:, :] = jnp.zeros((8 - HEADS, width), F32)
 
     def fill_early():
         for n in range(gtok_scr.shape[1] // width):
@@ -813,57 +847,61 @@
                 fill_early()
             action()
 
-        pl.when(step == min(samples + 2 * n, last))(run)
-
-    @pl.when(step == last)
-    def _():
-        lines = pair_gradient(pair_ref, score_scr, per, pair_chunk, blocks)
-        collect(edges(samples - 1))
-        weave(tail_stages(samples - 1))
+        pl.when(step == min(samples + 1 + 2 * n, last))(run)
+
+    def small_copies(k):
+        axis, count = axes[k]
+        base = 0 if k == 0 else axes[0][1] - 1
+        return [
+            pltpu.make_async_remote_copy(
+                src_ref=small_src.at[k],
+                dst_ref=(small_a, small_b)[k].at[d - 1],
+                send_sem=small_send.at[base + d - 1],
+                recv_sem=small_recv.at[base + d - 1],
+                device_id={axis: shifted_index(axis, count, d)},
+                device_id_type=MESH,
+            )
+            for d in range(1, count)
+        ]
+
+    def small_total(k):
+        value = small_src[k]
+        for n, copy in enumerate(small_copies(k)):
+            copy.wait()
+            value = value + (small_a, small_b)[k][n]
+        return value
+
+    def late_start():
+        for s in range(samples - LAG, samples):
+            collect(edges(s))
+            weave(weight_stages(s))
         for n in range(4):
             late_buf[n * width : (n + 1) * width, :] = gw_scr[:, n * width : (n + 1) * width]
         if late_buf.shape[0] > 4 * width:
             late_buf[4 * width :, :] = jnp.zeros((late_buf.shape[0] - 4 * width, width), F32)
-        acts = late.actions()
-        acts[0]()
-        small_src[0] = jnp.concatenate(
-            lines + [ggain_scr[...], jnp.zeros((8 - HEADS - 1, width), F32)], axis=0
-        )
-
-        def small_copies(k):
-            axis, count = axes[k]
-            base = 0 if k == 0 else axes[0][1] - 1
-            return [
-                pltpu.make_async_remote_copy(
-                    src_ref=small_src.at[k],
-                    dst_ref=(small_a, small_b)[k].at[d - 1],
-                    send_sem=small_send.at[base + d - 1],
-                    recv_sem=small_recv.at[base + d - 1],
-                    device_id={axis: shifted_index(axis, count, d)},
-                    device_id_type=MESH,
-                )
-                for d in range(1, count)
-            ]
-
+        late.scatter(0)
         for copy in small_copies(0):
             copy.start()
-        acts[1]()
-        value = small_src[0]
-        for n, copy in enumerate(small_copies(0)):
-            copy.wait()
-            value = value + small_a[n]
-        small_src[1] = value
+
+    def late_second():
+        late.scatter(1)
+        small_src[1] = small_total(0)
         for copy in small_copies(1):
             copy.start()
-        acts[2]()
-        for n, copy in enumerate(small_copies(1)):
-            copy.wait()
-            value = value + small_b[n]
-        small_ref[...] = value
-        acts[3]()
+
+    def late_third():
+        late.gather(1)
+        small_ref[...] = small_total(1)
+
+    def late_end():
+        late.finish()
         early_ref[...] = early_sum[...]
-        acts[4]()
         late_ref[...] = late_sum[...]
+
+    late_actions = [late_start, late_second, late_third, lambda: late.gather(0), late_end]
+    for n, action in enumerate(late_actions):
+        at = last if n == len(late_actions) - 1 else min(2 * samples + 2 + 2 * n, last)
+        pl.when(step == at)(action)
 
 
 def unpack_kernel(
@@ -871,6 +909,11 @@
     early_ref,
     late_ref,
     small_ref,
+    gain_ref,
+    wq_ref,
+    wk_ref,
+    wv_ref,
+    wg_ref,
     ggain_out,
     gq_out,
     gk_out,
@@ -889,10 +932,15 @@
     for n in range(blocks):
         gtok_out[:, n * width : (n + 1) * width] = block(early_ref, n)
     gout_out[...] = block(early_ref, blocks)
-    for n, ref in enumerate((gq_out, gk_out, gv_out, gg_out)):
-        ref[...] = block(late_ref, n)
+    by_gain = None
+    weights = (wq_ref, wk_ref, wv_ref, wg_ref)
+    for n, (ref, weight) in enumerate(zip((gq_out, gk_out, gv_out, gg_out), weights)):
+        grad = block(late_ref, n)
+        ref[...] = grad
+        part = grad * weight[...].astype(F32)
+        by_gain = part if by_gain is None else by_gain + part
+    ggain_out[...] = jnp.sum(by_gain.T, axis=0, keepdims=True) / gain_ref[...]
     lines = small_ref[...]
-    ggain_out[...] = lines[HEADS : HEADS + 1]
     shift = width // 2
     while shift >= channels:
         lines = lines + pltpu.roll(lines, shift, 1)
@@ -957,11 +1005,11 @@
         return jnp.clip(x, 0, samples - 1)
 
     def again(i):
-        return jnp.where(i <= samples, clip(i - 1), clip(i - samples - 1))
+        return jnp.where(i <= samples, clip(i - 1), clip(i - 2 * samples))
 
     pooled, gatoms, early, late, small = pl.pallas_call(
         functools.partial(step_kernel, samples, early_streams, late_streams),
-        grid=(2 * samples + 1,),
+        grid=(3 * samples,),
         in_specs=[
             pl.BlockSpec(memory_space=pltpu.SMEM),
             pl.BlockSpec(memory_space=pl.ANY),
@@ -974,14 +1022,14 @@
             square,
             square,
             whole(width, token_width),
-            whole(*w_pair.shape),
+            whole(*w_pair.T.shape),
             whole(*pair2.shape),
             whole(1, rows),
             pl.BlockSpec((1, tokens, token_width), lambda i: (clip(i - 1), 0, 0)),
         ],
         out_specs=[
             pl.BlockSpec((1, tokens, token_width), lambda i: (clip(i - 1), 0, 0)),
-            pl.BlockSpec((1, rows, width), lambda i: (clip(i - samples - 1), 0, 0)),
+            pl.BlockSpec((1, rows, width), lambda i: (clip(i - 2 * samples), 0, 0)),
             whole(early_total, width),
             whole(late_total, width),
             whole(8, width),
@@ -1006,21 +1054,19 @@
             vmem((width, 2 * width), BF16),
             vmem((width, 2 * width), BF16),
             vmem((width, 4 * width), BF16),
-            vmem((rows + 2 * rim, width), BF16),
+            vmem((samples, rows + 2 * rim, width), BF16),
             vmem((rows, width), F32),
             vmem((2, rows, width), BF16),
-            vmem((2, 3, rows, width), F32),
+            vmem((2, 2, rows, width), F32),
             vmem((samples, rows, width), BF16),
             vmem((samples, rows + 2 * rim, 2 * width), BF16),
             vmem((samples, blocks, KWIN, LANES), BF16),
-            vmem((samples, rows, 2 * width), BF16),
             vmem((samples, rows, width), BF16),
             vmem((samples, rows, width), BF16),
-            vmem((2, rows, 4 * width), BF16),
+            vmem((samples, rows, 4 * width), BF16),
             vmem((width, width), F32),
             vmem((width, token_width), F32),
             vmem((width, 4 * width), F32),
-            vmem((1, width), F32),
             vmem((early_total, width), F32),
             vmem((late_total, width), F32),
             vmem((early_total, width), BF16),
@@ -1059,7 +1105,7 @@
         w_gate,
         w_out,
         w_token,
-        w_pair,
+        w_pair.T,
         pair2,
         ids2,
         pooled_cot,
@@ -1067,12 +1113,12 @@
     spec = pl.BlockSpec(memory_space=pltpu.VMEM)
     ggain, gq, gk, gv, gg, gout, gtok, gpair = pl.pallas_call(
         functools.partial(unpack_kernel, channels),
-        in_specs=[spec] * 3,
+        in_specs=[spec] * 8,
         out_specs=[spec] * 8,
         out_shape=[shape((1, width), F32)]
         + [shape((width, width), F32)] * 5
         + [shape((width, token_width), F32), shape((HEADS, channels), F32)],
-    )(early, late, small)
+    )(early, late, small, gain2, w_query, w_key, w_value, w_gate)
     return (pooled, gatoms, ggain.reshape(width), gq, gk, gv, gg, gout, gtok, gpair.T)
 
 

time: 137 us -> 97 us (0.71)
  Pallas kernels: 132 us -> 92.7 us
    pallas_call x1, Pallas kernels: 130 us -> 90.6 us  [on_device(): pl.pallas_call(functools.partial(step_kernel, samples, early_streams, lat...]
    unnamed x5 -> x4, local copies, waits for them, and re-layouts: 4.64 us -> 3.28 us
where the time goes in v2:
time: 97 us; the launch traced here: 96.6 us
  Pallas kernels  92.7 us (96%)
  local copies, waits for them, and re-layouts  3.28 us (3%)
    pallas_call x1, Pallas kernels, on_device(): pl.pallas_call(functools.partial(step_kernel, samples, early_streams, lat...  90.6 us
    unnamed x4, local copies, waits for them, and re-layouts  3.28 us
    pallas_call x1, Pallas kernels, on_device(): pl.pallas_call(functools.partial(unpack_kernel, channels), in_specs=[spec...  2.07 us

profile of v2, /device:TPU:0, one launch (start us, length us, event | category | flops | bytes accessed | tf_op | source)
XLA Modules:
  0.0 96.6 jit_solution(4685307174743890034)
XLA Ops:
  0.6 90.6 %shard_map.204 = (bf16[12,48,768]{2,1,0:T(8,128)(2,1)}, bf16[12,512,128]{2,1,0:T(8,128)(2,1)}, bf16[1024,128]{1,0:T(8,128)(2,1)}, bf16[512,128]{1,0:T(8,128)(2,1)}, f32[8,128]{1,0:T(8,128)}) custom-call(s32[8]{0:T(128)} %counts_ref.1, bf16[12,512,128]{2,1,0:T(8,128)(2,1)} %again_ref.1, bf16[12,512,128]{2,1,0:T(8,128)(2,1)} %again_ref.1, ...), custom_call_target="tpu_custom_call" | custom-call | tf_op jit(solution)/shard_map/pallas_call | solution.py:1010
  91.2 0.0 copy-start
  91.3 2.1 %shard_map.205 = (f32[1,128]{1,0:T(1,128)}, f32[128,128]{1,0:T(8,128)}, f32[128,128]{1,0:T(8,128)}, f32[128,128]{1,0:T(8,128)}, f32[128,128]{1,0:T(8,128)}, /*in...) custom-call(bf16[1024,128]{1,0:T(8,128)(2,1)} %get-tuple-element.25.early_ref, ...), custom_call_target="tpu_custom_call" | custom-call | tf_op jit(solution)/shard_map/pallas_call | solution.py:1114
  93.3 2.1 %copy.25 = bf16[12,48,768]{2,1,0:T(8,128)(2,1)} copy(bf16[12,48,768]{2,1,0:T(8,128)(2,1)} %get-tuple-element.46) | data formatting | bytes 1769472
  95.5 0.0 copy-done
  95.5 1.1 %copy.26 = bf16[12,512,128]{2,1,0:T(8,128)(2,1)} copy(bf16[12,512,128]{2,1,0:T(8,128)(2,1)S(1)} %copy-done) | data formatting | bytes 3145728
Async XLA Ops:
  91.2 4.2 %copy-start = (bf16[12,512,128]{2,1,0:T(8,128)(2,1)S(1)}, bf16[12,512,128]{2,1,0:T(8,128)(2,1)}, u32[]{:S(2)}) copy-start(bf16[12,512,128]{2,1,0:T(8,128)(2,1)} %get-tuple-element.47) | copy-start | bytes 4718596

commit v3 on v2

--- a/solution.py
+++ b/solution.py
@@ -19,11 +19,14 @@
 NT = (((1,), (1,)), ((), ()))
 TN = (((0,), (0,)), ((), ()))
 GROUP = 4
-FGROUP = 4
+FGROUP = 8
 PARTS = 2
+BGROUP = 8
 LANES = 128
 MESH = pl.DeviceIdType.MESH
 LAG = 3
+EARLY_AT = (1, 4, 8, 12, 1 << 20)
+LATE_AT = (2, 5, 7, 9, 1 << 20)
 
 
 def mm(a, b, dims=NN):
@@ -350,7 +353,7 @@
     size = lax.axis_size("seq")
     last = 3 * samples - 1
 
-    early_orders = [axes[::-1] if s % 2 == 1 else axes for s in range(early_streams)]
+    early_orders = [axes] * early_streams
     early = Summer(
         early_buf,
         early_sum,
@@ -390,8 +393,11 @@
             device_id_type=MESH,
         )
 
+    halo_cuts = ((0, 1), (1, 2), (3, samples - 3))
+
     def halo(part):
-        span = pl.ds(0, 1) if part == 0 else pl.ds(1, samples - 1)
+        first, count = halo_cuts[part]
+        span = pl.ds(first, count)
         right = to_right(
             atoms_hbm.at[span, rows - rim : rows, :],
             low_in.at[span],
@@ -512,12 +518,12 @@
 
             return run
 
-        stages.append(rims)
         stages.append(norm(0))
         for c in range(cuts):
             if c + 1 < cuts:
                 stages.append(norm(c + 1))
             stages.append(project(c))
+        own = len(stages)
         groups = [[g * FGROUP + w for w in range(FGROUP)] for g in range(blocks // FGROUP)]
         count = len(groups)
         for g in range(count + 2):
@@ -527,7 +533,7 @@
                 stages.append(soften(g - 1, groups[g - 1]))
             if 0 <= g - 2 < count:
                 stages.append(attend(groups[g - 2]))
-        return stages
+        return [rims], stages[:own], stages[own:]
 
     def token_stages(s):
         slot = lax.rem(s, 2)
@@ -646,52 +652,64 @@
                 else:
                     opened.append(part)
 
-        def grads(g, spans):
+        def enter(g, spans):
             def run():
                 ges = [expand(gatt_all[s, b * QBLK : (b + 1) * QBLK, :], masks) for b in spans]
-                gps = [
+                held["gp", g] = [
                     mm(kv_all[s, b * QBLK : b * QBLK + KWIN, width:], ge, NT)
                     for b, ge in zip(spans, ges)
                 ]
+                held["dv", g] = [mm(low_all[s, b], ge) for b, ge in zip(spans, ges)]
+
+            return run
+
+        def middle(g, spans):
+            def run():
                 ps = [low_all[s, b].astype(F32) for b in spans]
-                ts = [p * gp for p, gp in zip(ps, gps)]
+                ts = [p * gp for p, gp in zip(ps, held.pop(("gp", g)))]
                 sums = [jnp.sum(t, axis=0, keepdims=True) for t in ts]
                 dss = [t - p * total for p, t, total in zip(ps, ts, sums)]
                 for b, ds in zip(spans, dss):
                     score_scr[b] += ds
-                held[g] = [ds.astype(BF16) for ds in dss]
-                held[g, "dv"] = [mm(low_all[s, b], ge) for b, ge in zip(spans, ges)]
+                held["ds", g] = [ds.astype(BF16) for ds in dss]
 
             return run
 
         def products(g, spans):
             def run():
-                lows = held.pop(g)
-                dvs = held.pop((g, "dv"))
+                lows = held.pop(("ds", g))
                 q_exp = [expand(q_all[s, b * QBLK : (b + 1) * QBLK, :], masks) for b in spans]
-                dks = [mm(low, q) for low, q in zip(lows, q_exp)]
-                dqs = [
+                held["dk", g] = [mm(low, q) for low, q in zip(lows, q_exp)]
+                held["dq", g] = [
                     mm(low, kv_all[s, b * QBLK : b * QBLK + KWIN, :width], TN)
                     for b, low in zip(spans, lows)
                 ]
-                for b, dk, dv in zip(spans, dks, dvs):
+
+            return run
+
+        def settle(g, spans):
+            def run():
+                for b, dk, dv in zip(spans, held.pop(("dk", g)), held.pop(("dv", g))):
                     merge(open_k, tiles(dk))
                     merge(open_v, tiles(dv))
                     close(b, 1)
-                for b, dq in zip(spans, dqs):
+                for b, dq in zip(spans, held.pop(("dq", g))):
                     d_all[s, b * QBLK : (b + 1) * QBLK, :width] = (
                         collapse(dq, lane_head) * scaling
                     ).astype(BF16)
 
             return run
 
-        group = 2
-        groups = [[g * group + w for w in range(group)] for g in range(blocks // group)]
-        stages.append(grads(0, groups[0]))
-        for g in range(len(groups)):
-            if g + 1 < len(groups):
-                stages.append(grads(g + 1, groups[g + 1]))
-            stages.append(products(g, groups[g]))
+        groups = [[g * BGROUP + w for w in range(BGROUP)] for g in range(blocks // BGROUP)]
+        count = len(groups)
+        for g in range(count + 2):
+            for lag, make in enumerate((enter, middle)):
+                if 0 <= g - lag < count:
+                    stages.append(make(g - lag, groups[g - lag]))
+            if 0 <= g - 1 < count:
+                stages.append(products(g - 1, groups[g - 1]))
+            if 0 <= g - 2 < count:
+                stages.append(settle(g - 2, groups[g - 2]))
         stages.append(lambda: close(blocks, len(open_k)))
         return stages
 
@@ -776,9 +794,6 @@
             high_in[...] = jnp.zeros_like(high_in)
             edge_in[1] = jnp.zeros_like(edge_in[1])
 
-        pl.semaphore_wait(barrier, sum(count - 1 for _, count in axes))
-        for part in range(2):
-            launch(halo(part))
         build_bias(
             counts_ref, pair_ref, pair_weights(wpair_ref, per), bias_scr, blocks, rows
         )
@@ -797,13 +812,21 @@
             wall_scr[:, n * width : (n + 1) * width] = ref[...]
         for ref in (score_scr, gout_scr, gtok_scr, gw_scr):
             ref[...] = jnp.zeros_like(ref)
+        pl.semaphore_wait(barrier, sum(count - 1 for _, count in axes))
+        for part in range(len(halo_cuts)):
+            launch(halo(part))
+        outer, own, rest = forward_stages(0)
+        weave(own)
         collect(halo(0))
-        weave(forward_stages(0))
-        collect(halo(1))
+        weave(outer + rest)
+
+    for part in range(1, len(halo_cuts)):
+        pl.when(step == halo_cuts[part][0])(lambda part=part: collect(halo(part)))
 
     @pl.when((step > 0) & (step < samples))
     def _():
-        weave(token_stages(step - 1), forward_stages(step))
+        outer, own, rest = forward_stages(step)
+        weave(token_stages(step - 1), outer + own + rest)
 
     @pl.when(step == samples)
     def _():
@@ -826,7 +849,7 @@
     def _():
         weave(finish_stages(step - 2 * samples))
 
-    @pl.when(step == 2 * samples)
+    @pl.when(step == min(2 * samples + 3, last))
     def _():
         lines = pair_gradient(pair_ref, score_scr, per, pair_chunk, blocks)
         for n, line in enumerate(lines):
@@ -847,7 +870,7 @@
                 fill_early()
             action()
 
-        pl.when(step == min(samples + 1 + 2 * n, last))(run)
+        pl.when(step == min(samples + EARLY_AT[n], last))(run)
 
     def small_copies(k):
         axis, count = axes[k]
@@ -880,17 +903,20 @@
         if late_buf.shape[0] > 4 * width:
             late_buf[4 * width :, :] = jnp.zeros((late_buf.shape[0] - 4 * width, width), F32)
         late.scatter(0)
+
+    def late_second():
         for copy in small_copies(0):
             copy.start()
-
-    def late_second():
         late.scatter(1)
+
+    def late_third():
+        late.gather(1)
         small_src[1] = small_total(0)
         for copy in small_copies(1):
             copy.start()
 
-    def late_third():
-        late.gather(1)
+    def late_fourth():
+        late.gather(0)
         small_ref[...] = small_total(1)
 
     def late_end():
@@ -898,10 +924,9 @@
         early_ref[...] = early_sum[...]
         late_ref[...] = late_sum[...]
 
-    late_actions = [late_start, late_second, late_third, lambda: late.gather(0), late_end]
+    late_actions = [late_start, late_second, late_third, late_fourth, late_end]
     for n, action in enumerate(late_actions):
-        at = last if n == len(late_actions) - 1 else min(2 * samples + 2 + 2 * n, last)
-        pl.when(step == at)(action)
+        pl.when(step == min(2 * samples + LATE_AT[n], last))(action)
 
 
 def unpack_kernel(
@@ -914,6 +939,8 @@
     wk_ref,
     wv_ref,
     wg_ref,
+    pooled_ref,
+    gatoms_ref,
     ggain_out,
     gq_out,
     gk_out,
@@ -922,13 +949,38 @@
     gout_out,
     gtok_out,
     gpair_out,
+    pooled_out,
+    gatoms_out,
+    pooled_scr,
+    gatoms_scr,
+    sems,
 ):
+    moves = []
+    count = sems.shape[0] // 4
+    for n, (src, mid, dst) in enumerate(
+        ((pooled_ref, pooled_scr, pooled_out), (gatoms_ref, gatoms_scr, gatoms_out))
+    ):
+        size = src.shape[0] // count
+        for c in range(count):
+            span = pl.ds(c * size, size)
+            at = 2 * (n * count + c)
+            moves.append(
+                (
+                    pltpu.make_async_copy(src.at[span], mid.at[span], sems.at[at]),
+                    pltpu.make_async_copy(mid.at[span], dst.at[span], sems.at[at + 1]),
+                )
+            )
+    for fetch, _ in moves:
+        fetch.start()
     width = gout_out.shape[0]
     blocks = gtok_out.shape[1] // width
 
     def block(ref, n):
         return ref[n * width : (n + 1) * width, :].astype(F32)
 
+    for fetch, put in moves:
+        fetch.wait()
+        put.start()
     for n in range(blocks):
         gtok_out[:, n * width : (n + 1) * width] = block(early_ref, n)
     gout_out[...] = block(early_ref, blocks)
@@ -946,6 +998,8 @@
         lines = lines + pltpu.roll(lines, shift, 1)
         shift //= 2
     gpair_out[...] = lines[:HEADS, :channels]
+    for _, put in moves:
+        put.wait()
 
 
 def whole(*shape):
@@ -999,7 +1053,7 @@
     late_total = -(-(4 * width) // unit) * unit
     early_streams = early_total // unit
     late_streams = late_total // unit
-    early_orders = [axes[::-1] if s % 2 == 1 else axes for s in range(early_streams)]
+    early_orders = [axes] * early_streams
 
     def clip(x):
         return jnp.clip(x, 0, samples - 1)
@@ -1074,8 +1128,8 @@
             vmem((axes[0][1] - 1, 8, width), F32),
             vmem((axes[1][1] - 1, 8, width), F32),
             vmem((2, 8, width), F32),
-            dma((2, 2)),
-            dma((2, 2)),
+            dma((2, 3)),
+            dma((2, 3)),
             dma((2, samples)),
             dma((2, samples)),
             dma((2 * early_streams * peers,)),
@@ -1111,14 +1165,18 @@
         pooled_cot,
     )
     spec = pl.BlockSpec(memory_space=pltpu.VMEM)
-    ggain, gq, gk, gv, gg, gout, gtok, gpair = pl.pallas_call(
+    anywhere = pl.BlockSpec(memory_space=pl.ANY)
+    pieces = next(n for n in (4, 3, 2, 1) if samples % n == 0)
+    ggain, gq, gk, gv, gg, gout, gtok, gpair, pooled, gatoms = pl.pallas_call(
         functools.partial(unpack_kernel, channels),
-        in_specs=[spec] * 8,
-        out_specs=[spec] * 8,
+        in_specs=[spec] * 8 + [anywhere] * 2,
+        out_specs=[spec] * 8 + [anywhere] * 2,
         out_shape=[shape((1, width), F32)]
         + [shape((width, width), F32)] * 5
-        + [shape((width, token_width), F32), shape((HEADS, channels), F32)],
-    )(early, late, small, gain2, w_query, w_key, w_value, w_gate)
+        + [shape((width, token_width), F32), shape((HEADS, channels), F32)]
+        + [shape(pooled.shape, BF16), shape(gatoms.shape, BF16)],
+        scratch_shapes=[vmem(pooled.shape, BF16), vmem(gatoms.shape, BF16), dma((4 * pieces,))],
+    )(early, late, small, gain2, w_query, w_key, w_value, w_gate, pooled, gatoms)
     return (pooled, gatoms, ggain.reshape(width), gq, gk, gv, gg, gout, gtok, gpair.T)
 
 

time: 97 us -> 87 us (0.90)
  Pallas kernels: 92.7 us -> 86 us
  local copies, waits for them, and re-layouts: 3.28 us -> 0 us
    pallas_call x1, Pallas kernels: 90.6 us -> 81.4 us  [on_device(): pl.pallas_call(functools.partial(step_kernel, samples, early_streams, lat...]
    unnamed x4 -> x0, local copies, waits for them, and re-layouts: 3.28 us -> none
    pallas_call x1, Pallas kernels: 2.07 us -> 4.6 us  [on_device(): pl.pallas_call(functools.partial(unpack_kernel, channels), in_specs=[spec...]
where the time goes in v3:
time: 87 us; the launch traced here: 86.7 us
  Pallas kernels  86 us (99%)
    pallas_call x1, Pallas kernels, on_device(): pl.pallas_call(functools.partial(step_kernel, samples, early_streams, lat...  81.4 us
    pallas_call x1, Pallas kernels, on_device(): pl.pallas_call(functools.partial(unpack_kernel, channels), in_specs=[spec...  4.6 us

profile of v3, /device:TPU:0, one launch (start us, length us, event | category | flops | bytes accessed | tf_op | source)
XLA Modules:
  0.0 86.7 jit_solution(1181703288587346059)
XLA Ops:
  0.6 81.4 %shard_map.204 = (bf16[12,48,768]{2,1,0:T(8,128)(2,1)}, bf16[12,512,128]{2,1,0:T(8,128)(2,1)}, bf16[1024,128]{1,0:T(8,128)(2,1)}, bf16[512,128]{1,0:T(8,128)(2,1)}, f32[8,128]{1,0:T(8,128)}) custom-call(s32[8]{0:T(128)} %counts_ref.1, bf16[12,512,128]{2,1,0:T(8,128)(2,1)} %again_ref.1, bf16[12,512,128]{2,1,0:T(8,128)(2,1)} %again_ref.1, ...), custom_call_target="tpu_custom_call" | custom-call | tf_op jit(solution)/shard_map/pallas_call | solution.py:1064
  82.1 4.6 %shard_map.205 = (f32[1,128]{1,0:T(1,128)}, f32[128,128]{1,0:T(8,128)}, f32[128,128]{1,0:T(8,128)}, f32[128,128]{1,0:T(8,128)}, f32[128,128]{1,0:T(8,128)}, /*in...) custom-call(bf16[1024,128]{1,0:T(8,128)(2,1)} %get-tuple-element.25., ...), custom_call_target="tpu_custom_call" | custom-call | tf_op jit(solution)/shard_map/pallas_call | solution.py:1170

commit v4 on v3

--- a/solution.py
+++ b/solution.py
@@ -20,7 +20,7 @@
 TN = (((0,), (0,)), ((), ()))
 GROUP = 4
 FGROUP = 8
-PARTS = 2
+PARTS = 1
 BGROUP = 8
 LANES = 128
 MESH = pl.DeviceIdType.MESH
@@ -286,7 +286,7 @@
     wo_ref,
     wt_ref,
     wpair_ref,
-    pair_ref,
+    pair_hbm,
     ids_ref,
     cot_ref,
     pooled_ref,
@@ -298,6 +298,7 @@
     high_in,
     edge_out,
     edge_in,
+    pair_ref,
     bias_scr,
     score_scr,
     member_scr,
@@ -306,6 +307,7 @@
     wqg_scr,
     wkv_scr,
     wall_scr,
+    half_scr,
     hid_all,
     gate_scr,
     gated_scr,
@@ -336,6 +338,7 @@
     late_recv,
     small_send,
     small_recv,
+    pair_sem,
     *slots,
 ):
     step = pl.program_id(0)
@@ -546,7 +549,7 @@
             gated = gated_scr[slot]
             x = again_ref[0].astype(F32)
             held["updated"] = (x + mm(gated, wo_ref[...])).astype(BF16)
-            held["cot"] = (cot_ref[0].astype(F32) * inv_scr[...]).astype(BF16)
+            held["cot"] = (cot_ref[0].astype(F32) * (0.5 * inv_scr[...])).astype(BF16)
             held["gupd"] = [None, None]
 
         def enter(c, r):
@@ -554,7 +557,7 @@
                 cols = slice(c * chunk, (c + 1) * chunk)
                 span = slice(r * half, (r + 1) * half)
                 held[c, r] = (
-                    mm(held["updated"][span], wt_ref[:, cols]),
+                    mm(held["updated"][span], half_scr[:, cols]),
                     mm(member_scr[span, :], held["cot"][:, cols]),
                     [],
                     [],
@@ -567,10 +570,11 @@
                 pre, grad_act, acts, grads = held[c, r]
                 part = slice(n * half // PARTS, (n + 1) * half // PARTS)
                 pre, grad_act = pre[part], grad_act[part]
-                sig = sigmoid(pre)
-                value = pre * sig
+                bent = jnp.tanh(pre)
+                rise = 1.0 + bent
+                value = pre * rise
                 acts.append(value.astype(BF16))
-                grads.append((grad_act * (sig + value * (1.0 - sig))).astype(BF16))
+                grads.append((grad_act * (rise + value * (1.0 - bent))).astype(BF16))
 
             return run
 
@@ -714,7 +718,7 @@
         return stages
 
     def weight_stages(s):
-        cuts = 2
+        cuts = 1
         chunk = rows // cuts
 
         def join():
@@ -784,6 +788,9 @@
                     device_id_type=MESH,
                 )
 
+        pair_copy = pltpu.make_async_copy(pair_hbm, pair_ref, pair_sem.at[0])
+        pair_copy.start()
+
         @pl.when(pos == 0)
         def _():
             low_in[...] = jnp.zeros_like(low_in)
@@ -794,9 +801,6 @@
             high_in[...] = jnp.zeros_like(high_in)
             edge_in[1] = jnp.zeros_like(edge_in[1])
 
-        build_bias(
-            counts_ref, pair_ref, pair_weights(wpair_ref, per), bias_scr, blocks, rows
-        )
         token = lax.broadcasted_iota(jnp.int32, (tokens, rows), 0)
         place = lax.broadcasted_iota(jnp.int32, (tokens, rows), 1)
         hit = (ids_ref[...] - pos * tokens == token) & (place < counts_ref[pos])
@@ -804,6 +808,7 @@
         inv_scr[...] = 1.0 / jnp.sum(member_t, axis=1, keepdims=True)
         member_t_scr[...] = member_t.astype(BF16)
         member_scr[...] = member_t.T.astype(BF16)
+        half_scr[...] = (0.5 * wt_ref[...].astype(F32)).astype(BF16)
         wqg_scr[:, :width] = wq_ref[...]
         wqg_scr[:, width:] = wg_ref[...]
         wkv_scr[:, :width] = wk_ref[...]
@@ -812,6 +817,10 @@
             wall_scr[:, n * width : (n + 1) * width] = ref[...]
         for ref in (score_scr, gout_scr, gtok_scr, gw_scr):
             ref[...] = jnp.zeros_like(ref)
+        pair_copy.wait()
+        build_bias(
+            counts_ref, pair_ref, pair_weights(wpair_ref, per), bias_scr, blocks, rows
+        )
         pl.semaphore_wait(barrier, sum(count - 1 for _, count in axes))
         for part in range(len(halo_cuts)):
             launch(halo(part))
@@ -1077,7 +1086,7 @@
             square,
             whole(width, token_width),
             whole(*w_pair.T.shape),
-            whole(*pair2.shape),
+            pl.BlockSpec(memory_space=pl.ANY),
             whole(1, rows),
             pl.BlockSpec((1, tokens, token_width), lambda i: (clip(i - 1), 0, 0)),
         ],
@@ -1100,6 +1109,7 @@
             vmem((samples, rim, width), BF16),
             vmem((2, samples, rim, 2 * width), BF16),
             vmem((2, samples, rim, 2 * width), BF16),
+            vmem(pair2.shape, BF16),
             vmem((blocks, KWIN, LANES), F32),
             vmem((blocks, KWIN, LANES), F32),
             vmem((rows, tokens), BF16),
@@ -1108,6 +1118,7 @@
             vmem((width, 2 * width), BF16),
             vmem((width, 2 * width), BF16),
             vmem((width, 4 * width), BF16),
+            vmem((width, token_width), BF16),
             vmem((samples, rows + 2 * rim, width), BF16),
             vmem((rows, width), F32),
             vmem((2, rows, width), BF16),
@@ -1138,6 +1149,7 @@
             dma((2 * late_streams * peers,)),
             dma((peers,)),
             dma((peers,)),
+            dma((1,)),
         ]
         + sum_scratch(early_total, early_streams, early_orders, width)
         + sum_scratch(late_total, late_streams, [axes] * late_streams, width),

time: 87 us -> 86.3 us (level)
  no operation moved by 1% of the time
where the time goes in v4:
time: 86.3 us; the launch traced here: 86 us
  Pallas kernels  85.3 us (99%)
    pallas_call x1, Pallas kernels, on_device(): pl.pallas_call(functools.partial(step_kernel, samples, early_streams, lat...  80.7 us
    pallas_call x1, Pallas kernels, on_device(): pl.pallas_call(functools.partial(unpack_kernel, channels), in_specs=[spec...  4.6 us

profile of v4, /device:TPU:0, one launch (start us, length us, event | category | flops | bytes accessed | tf_op | source)
XLA Modules:
  0.0 86.0 jit_solution(7493020914478148959)
XLA Ops:
  0.6 80.7 %shard_map.204 = (bf16[12,48,768]{2,1,0:T(8,128)(2,1)}, bf16[12,512,128]{2,1,0:T(8,128)(2,1)}, bf16[1024,128]{1,0:T(8,128)(2,1)}, bf16[512,128]{1,0:T(8,128)(2,1)}, f32[8,128]{1,0:T(8,128)}) custom-call(s32[8]{0:T(128)} %counts_ref.1, bf16[12,512,128]{2,1,0:T(8,128)(2,1)} %again_ref.1, bf16[12,512,128]{2,1,0:T(8,128)(2,1)} %again_ref.1, ...), custom_call_target="tpu_custom_call" | custom-call | tf_op jit(solution)/shard_map/pallas_call | solution.py:1073
  81.4 4.6 %shard_map.205 = (f32[1,128]{1,0:T(1,128)}, f32[128,128]{1,0:T(8,128)}, f32[128,128]{1,0:T(8,128)}, f32[128,128]{1,0:T(8,128)}, f32[128,128]{1,0:T(8,128)}, /*in...) custom-call(bf16[1024,128]{1,0:T(8,128)(2,1)} %get-tuple-element.25., ...), custom_call_target="tpu_custom_call" | custom-call | tf_op jit(solution)/shard_map/pallas_call | solution.py:1182

commit v5 on v4

--- a/solution.py
+++ b/solution.py
@@ -938,37 +938,25 @@
         pl.when(step == min(2 * samples + LATE_AT[n], last))(action)
 
 
-def unpack_kernel(
-    channels,
-    early_ref,
-    late_ref,
-    small_ref,
-    gain_ref,
-    wq_ref,
-    wk_ref,
-    wv_ref,
-    wg_ref,
-    pooled_ref,
-    gatoms_ref,
-    ggain_out,
-    gq_out,
-    gk_out,
-    gv_out,
-    gg_out,
-    gout_out,
-    gtok_out,
-    gpair_out,
-    pooled_out,
-    gatoms_out,
-    pooled_scr,
-    gatoms_scr,
-    sems,
-):
+def unpack_kernel(channels, inputs, outputs, *refs):
+    ins, refs = refs[:inputs], refs[inputs:]
+    big_ins, refs = refs[:2], refs[2:]
+    outs, refs = refs[:outputs], refs[outputs:]
+    big_outs, refs = refs[:2], refs[2:]
+    held_ins, refs = refs[:inputs], refs[inputs:]
+    held_outs, refs = refs[:outputs], refs[outputs:]
+    big_held, (in_sems, out_sems, sems) = refs[:2], refs[2:]
+    loads = [
+        pltpu.make_async_copy(src, dst, in_sems.at[n])
+        for n, (src, dst) in enumerate(zip(ins, held_ins))
+    ]
+    stores = [
+        pltpu.make_async_copy(src, dst, out_sems.at[n])
+        for n, (src, dst) in enumerate(zip(held_outs, outs))
+    ]
     moves = []
     count = sems.shape[0] // 4
-    for n, (src, mid, dst) in enumerate(
-        ((pooled_ref, pooled_scr, pooled_out), (gatoms_ref, gatoms_scr, gatoms_out))
-    ):
+    for n, (src, mid, dst) in enumerate(zip(big_ins, big_held, big_outs)):
         size = src.shape[0] // count
         for c in range(count):
             span = pl.ds(c * size, size)
@@ -979,22 +967,25 @@
                     pltpu.make_async_copy(mid.at[span], dst.at[span], sems.at[at + 1]),
                 )
             )
+    for load in loads:
+        load.start()
     for fetch, _ in moves:
         fetch.start()
+    for load in loads:
+        load.wait()
+    early_ref, late_ref, small_ref, gain_ref = held_ins[:4]
+    weights = held_ins[4:]
+    ggain_out, gq_out, gk_out, gv_out, gg_out, gout_out, gtok_out, gpair_out = held_outs
     width = gout_out.shape[0]
     blocks = gtok_out.shape[1] // width
 
     def block(ref, n):
         return ref[n * width : (n + 1) * width, :].astype(F32)
 
-    for fetch, put in moves:
-        fetch.wait()
-        put.start()
     for n in range(blocks):
         gtok_out[:, n * width : (n + 1) * width] = block(early_ref, n)
     gout_out[...] = block(early_ref, blocks)
     by_gain = None
-    weights = (wq_ref, wk_ref, wv_ref, wg_ref)
     for n, (ref, weight) in enumerate(zip((gq_out, gk_out, gv_out, gg_out), weights)):
         grad = block(late_ref, n)
         ref[...] = grad
@@ -1007,6 +998,13 @@
         lines = lines + pltpu.roll(lines, shift, 1)
         shift //= 2
     gpair_out[...] = lines[:HEADS, :channels]
+    for store in stores:
+        store.start()
+    for fetch, put in moves:
+        fetch.wait()
+        put.start()
+    for store in stores:
+        store.wait()
     for _, put in moves:
         put.wait()
 
@@ -1176,19 +1174,23 @@
         ids2,
         pooled_cot,
     )
-    spec = pl.BlockSpec(memory_space=pltpu.VMEM)
     anywhere = pl.BlockSpec(memory_space=pl.ANY)
     pieces = next(n for n in (4, 3, 2, 1) if samples % n == 0)
-    ggain, gq, gk, gv, gg, gout, gtok, gpair, pooled, gatoms = pl.pallas_call(
-        functools.partial(unpack_kernel, channels),
-        in_specs=[spec] * 8 + [anywhere] * 2,
-        out_specs=[spec] * 8 + [anywhere] * 2,
-        out_shape=[shape((1, width), F32)]
+    operands = (early, late, small, gain2, w_query, w_key, w_value, w_gate)
+    results = (
+        [shape((1, width), F32)]
         + [shape((width, width), F32)] * 5
         + [shape((width, token_width), F32), shape((HEADS, channels), F32)]
-        + [shape(pooled.shape, BF16), shape(gatoms.shape, BF16)],
-        scratch_shapes=[vmem(pooled.shape, BF16), vmem(gatoms.shape, BF16), dma((4 * pieces,))],
-    )(early, late, small, gain2, w_query, w_key, w_value, w_gate, pooled, gatoms)
+    )
+    large = [shape(pooled.shape, BF16), shape(gatoms.shape, BF16)]
+    ggain, gq, gk, gv, gg, gout, gtok, gpair, pooled, gatoms = pl.pallas_call(
+        functools.partial(unpack_kernel, channels, len(operands), len(results)),
+        in_specs=[anywhere] * (len(operands) + 2),
+        out_specs=[anywhere] * (len(results) + 2),
+        out_shape=results + large,
+        scratch_shapes=[vmem(x.shape, x.dtype) for x in (*operands, *results, *large)]
+        + [dma((len(operands),)), dma((len(results),)), dma((4 * pieces,))],
+    )(*operands, pooled, gatoms)
     return (pooled, gatoms, ggain.reshape(width), gq, gk, gv, gg, gout, gtok, gpair.T)
 
 

time: 86.3 us -> 85.4 us (0.990)
  Pallas kernels: 85.3 us -> 84.4 us
    pallas_call x1, Pallas kernels: 4.6 us -> 3.68 us  [on_device(): pl.pallas_call(functools.partial(unpack_kernel, channels, len(operands),...]
where the time goes in v5:
time: 85.4 us; the launch traced here: 85.1 us
  Pallas kernels  84.4 us (99%)
    pallas_call x1, Pallas kernels, on_device(): pl.pallas_call(functools.partial(step_kernel, samples, early_streams, lat...  80.7 us
    pallas_call x1, Pallas kernels, on_device(): pl.pallas_call(functools.partial(unpack_kernel, channels, len(operands),...  3.68 us

profile of v5, /device:TPU:0, one launch (start us, length us, event | category | flops | bytes accessed | tf_op | source)
XLA Modules:
  0.0 85.1 jit_solution(14723757096680479426)
XLA Ops:
  0.6 80.7 %shard_map.204 = (bf16[12,48,768]{2,1,0:T(8,128)(2,1)}, bf16[12,512,128]{2,1,0:T(8,128)(2,1)}, bf16[1024,128]{1,0:T(8,128)(2,1)}, bf16[512,128]{1,0:T(8,128)(2,1)}, f32[8,128]{1,0:T(8,128)}) custom-call(s32[8]{0:T(128)} %counts_ref.1, bf16[12,512,128]{2,1,0:T(8,128)(2,1)} %again_ref.1, bf16[12,512,128]{2,1,0:T(8,128)(2,1)} %again_ref.1, ...), custom_call_target="tpu_custom_call" | custom-call | tf_op jit(solution)/shard_map/pallas_call | solution.py:1071
  81.4 3.7 %shard_map.205 = (f32[1,128]{1,0:T(1,128)}, f32[128,128]{1,0:T(8,128)}, f32[128,128]{1,0:T(8,128)}, f32[128,128]{1,0:T(8,128)}, f32[128,128]{1,0:T(8,128)}, /*in...) custom-call(bf16[1024,128]{1,0:T(8,128)(2,1)} %get-tuple-element.25., ...), custom_call_target="tpu_custom_call" | custom-call | tf_op jit(solution)/shard_map/pallas_call | solution.py:1186
